TPU v7x, 256 devices: a whole 4x4x8 slice. The times are simulated.
256 devices in a mesh: exp: 64 (over z, x, core), sub: 4 (over y).
Axes of the slice: x: 4, y: 4, z: 8, core: 2. Of those that a mesh axis runs over, the one named last changes fastest.
Arguments:
- sky_map: float32 [256, 8, 8, 128], P(('exp', 'sub')), may hold values from -6 to 6
- coeffs: bfloat16 [128, 12, 512, 512], P('exp', None, 'sub'), may hold values from -1.75 to 1.75
- observed: float32 [128, 512, 512], P('exp', 'sub'), may hold values from -6 to 6
- vert_taps: bfloat16 [12, 21], replicated, may hold values from -1.25 to 1.25
- horiz_taps: bfloat16 [12, 21], replicated, may hold values from -1.25 to 1.25
- owner_ids: int32 [128, 64, 4, 1], P('exp', 'sub'), may hold values from 0 to 63; in each aligned block of 64 rows (0 to 63, 64 to 127, ..., all dimensions but the last counted through in order) at most 2 rows name the same one
- offset: int32 [128, 64, 4], P('exp', 'sub'), may hold values from 0 to 7
Outputs:
- sky_final: float32 [256, 8, 8, 128], P(('exp', 'sub'))
- clipped: float32 [128, 512, 512], P('exp', 'sub')
Inputs may be any that keep to these rules, and one draw needn't show every extreme that they name: Patch (e, r, q) reads sky tile owner_ids[e, r, q, 0] * 4 + r // 16. Among the 64 patches of one band of one piece (the rows of one device's piece) no owner is named more than 2 times, and in every draw some band names one owner exactly 2 times.
All inputs are finite; a program needn't handle non-finite values.
Results may differ from a plain program's by a relative error of at most 0.0035.
Values may be sent and summed in bfloat16 or wider, within the bound.
A program may use at most 64 MiB of HBM per device.

v0:
```python
import jax
import jax.numpy as jnp
from jax import lax
from jax.sharding import PartitionSpec as P

STEPS = 2


ETA = 0.5
DELTA = 1.0


def padded_2(cells, sides, width):
    for axis, dim in sides:
        count = lax.axis_size(axis)
        ends = count - 1
        head = lax.slice_in_dim(cells, 0, width, axis=dim)
        tail = lax.slice_in_dim(cells, cells.shape[dim] - width, cells.shape[dim], axis=dim)
        cells = jnp.concatenate(
            [
                lax.ppermute(tail, axis, [(i, (i + 1) % count) for i in range(ends)]),
                cells,
                lax.ppermute(head, axis, [((i + 1) % count, i) for i in range(ends)]),
            ],
            axis=dim,
        )
    return cells


def from_behind(block, axis, distance):
    devices = range(lax.axis_size(axis))
    route = [(i - distance, i) for i in devices if i - distance in devices]
    return lax.ppermute(block, axis, route)


def band_table(filters, height, breadth, direction):
    row_ids = lax.broadcasted_iota(jnp.int32, (height, breadth), 0)
    col_ids = lax.broadcasted_iota(jnp.int32, (height, breadth), 1)
    lag_ids = direction * (col_ids - row_ids)
    tap_ids = lax.broadcasted_iota(jnp.int32, (filters.shape[1], height, breadth), 0)
    select = (tap_ids == lag_ids[None]).astype(jnp.float32)
    return jnp.einsum("mt,tij->mij", filters.astype(jnp.float32), select).astype(jnp.bfloat16)


def per_device(sky_map, coeffs, observed, vert_taps, horiz_taps, owner_ids, offset):
    pieces, height, breadth = observed.shape
    mode_count = coeffs.shape[1]
    per_tile = sky_map.shape[1]
    patch_rows = sky_map.shape[2]
    patch_cols = sky_map.shape[3]
    patch_size = patch_rows * patch_cols
    margin = (vert_taps.shape[1] - 1) // 2
    exp_count = lax.axis_size("exp")
    rows_band = height // patch_rows
    cols_band = breadth // patch_cols
    per_band = rows_band * cols_band
    requests = pieces * per_band
    vertical = band_table(vert_taps, height, height + 2 * margin, 1)
    horizontal = band_table(horiz_taps, patch_cols + 2 * margin, patch_cols, -1)
    owners = owner_ids.reshape(requests)
    offsets = offset.reshape(requests)
    all_ids = owners * per_tile + offsets
    table_f = (
        all_ids[:, None] == lax.broadcasted_iota(jnp.int32, (1, exp_count * per_tile), 1)
    ).astype(jnp.float32)
    table_b = table_f.astype(jnp.bfloat16)
    counts = lax.psum_scatter(
        jnp.sum(table_f, axis=0).reshape(exp_count, per_tile),
        "exp",
        scatter_dimension=0,
        tiled=True,
    ).reshape(per_tile)
    current = sky_map.reshape(per_tile, patch_size)
    clipped = jnp.zeros(observed.shape, jnp.float32)
    for step_index in range(STEPS):
        shard_piece = lax.all_gather(
            current.astype(jnp.bfloat16).reshape(1, per_tile, patch_size), "exp", axis=0, tiled=True
        )
        tile_count = shard_piece.shape[0]
        patches = jnp.dot(
            table_b,
            shard_piece.reshape(tile_count * per_tile, patch_size),
            preferred_element_type=jnp.float32,
        ).astype(jnp.bfloat16)
        to_stacked = patches.reshape(pieces, rows_band, cols_band, patch_rows, patch_cols)
        extended = padded_2(
            to_stacked.transpose(0, 1, 3, 2, 4).reshape(pieces, height, breadth),
            (("sub", 1),),
            margin,
        )
        smoothed = jnp.einsum(
            "mia,pac->pmic", vertical, extended, preferred_element_type=jnp.float32
        ).astype(jnp.bfloat16)
        padded = jnp.pad(smoothed, ((0, 0), (0, 0), (0, 0), (margin, margin)))
        windows = jnp.stack(
            [
                padded[
                    ...,
                    block_index * patch_cols : block_index * patch_cols + patch_cols + 2 * margin,
                ]
                for block_index in range(cols_band)
            ],
            axis=3,
        )
        blurred = jnp.einsum(
            "pmbkw,mwc->pmbkc", windows, horizontal, preferred_element_type=jnp.float32
        ).reshape(pieces, mode_count, height, breadth)
        modeled = jnp.sum(coeffs.astype(jnp.float32) * blurred, axis=1)
        evaluate_clipped = jnp.clip(modeled - observed, -DELTA, DELTA)
        weighted = (coeffs.astype(jnp.float32) * evaluate_clipped[:, None]).astype(jnp.bfloat16)
        spread = jnp.einsum(
            "pmbkc,mwc->pmbkw",
            weighted.reshape(pieces, mode_count, height, cols_band, patch_cols),
            horizontal,
            preferred_element_type=jnp.float32,
        )
        summed = jnp.zeros((pieces, mode_count, height, breadth + 2 * margin), jnp.float32)
        for block_index in range(cols_band):
            summed = summed + jnp.pad(
                spread[:, :, :, block_index],
                (
                    (0, 0),
                    (0, 0),
                    (0, 0),
                    (block_index * patch_cols, breadth - (block_index + 1) * patch_cols),
                ),
            )
        back_rows = summed[..., margin : margin + breadth].astype(jnp.bfloat16)
        gathered_rows = jnp.einsum(
            "mia,pmic->pac", vertical, back_rows, preferred_element_type=jnp.float32
        )
        upper_rim = gathered_rows[:, :margin]
        lower_rim = gathered_rows[:, height + margin :]
        from_below = from_behind(upper_rim, "sub", -1)
        from_above = from_behind(lower_rim, "sub", 1)
        gradient = gathered_rows[:, margin : margin + height]
        gradient = (
            gradient
            + jnp.pad(from_above, ((0, 0), (0, height - margin), (0, 0)))
            + jnp.pad(from_below, ((0, 0), (height - margin, 0), (0, 0)))
        )
        clipped, gradient = (evaluate_clipped, gradient)
        stacked = gradient.reshape(pieces, rows_band, patch_rows, cols_band, patch_cols)
        grad_patches = stacked.transpose(0, 1, 3, 2, 4).reshape(requests, patch_size)
        summed = lax.psum_scatter(
            lax.dot_general(
                table_f, grad_patches, (((0,), (0,)), ((), ())), precision=lax.Precision.HIGHEST
            ),
            "exp",
            scatter_dimension=0,
            tiled=True,
        )
        current = current - ETA * summed / jnp.maximum(counts, 1.0)[:, None]
    return (current.reshape(sky_map.shape), clipped)


def solution(mesh):
    return jax.shard_map(
        per_device,
        mesh=mesh,
        in_specs=(
            P(("exp", "sub"), None, None, None),
            P("exp", None, "sub", None),
            P("exp", "sub", None),
            P(),
            P(),
            P("exp", "sub", None, None),
            P("exp", "sub", None),
        ),
        out_specs=(P(("exp", "sub"), None, None, None), P("exp", "sub", None)),
        check_vma=False,
    )
```

profile of v0, /device:TPU:1, one launch (start us, length us, event | category | flops | bytes accessed | tf_op | source)
XLA Modules:
  0.0 715.6 jit_solution(18267638803737350568)
XLA Ops:
  7.2 0.8 convert_element_type.96
  8.0 0.6 convert_element_type.97
  8.6 0.0 all-reduce.20.cloned.1.call-start
  8.7 0.7 broadcast_multiply_fusion
  9.4 0.1 copy.84
  9.5 0.1 mul.53
  9.6 0.8 copy.85
  10.3 0.1 reshape.112
  10.5 0.5 fusion.26
  11.0 81.3 %all-gather.4.cloned.1.call-done = bf16[64,8,1024]{2,1,0:T(8,128)(2,1)} async-done(((bf16[1,8,1024]{2,1,0:T(8,128)(2,1)}), bf16[64,8,1024]{2,1,0:T(8,128)(2,1)}) %all-gather.4.cloned.1.call-update) | async-done | bytes 1048592 | tf_op jit(solution)/shard_map/all_gather | solution.py:76
  92.3 1.6 fusion.35
  94.0 3.1 collective-permute-start
  97.1 1.3 collective-permute-start.1
  98.4 1.2 fusion.34
  99.6 2.2 collective-permute-done.1
  101.7 1.0 convert_bitcast_fusion.1
  102.8 1.9 fusion.38
  104.7 3.3 fusion.8
  108.0 6.7 copy.89
  114.7 4.1 fusion
  118.9 0.1 subtract_clamp_fusion.1
  119.0 2.4 fusion.1
  121.4 5.5 reshape.117
  126.9 4.3 fusion.18
  131.3 0.6 slice_bitcast_fusion.7
  131.9 0.4 copy-done.6
  132.3 1.2 fusion.31
  133.6 3.1 collective-permute-start.2
  136.7 1.5 collective-permute-start.3
  138.2 3.5 collective-permute-done.3
  141.7 0.1 fusion.51
  141.8 2.4 fusion.47
  144.3 0.1 convert_reduce_fusion
  144.4 0.1 reshape.120
  144.5 0.6 dynamic-slice
  145.7 244.0 %all-reduce.15 = f32[64,8]{1,0:T(8,128)S(1)} all-reduce(f32[64,8]{1,0:T(8,128)S(1)} %reshape.120), channel_id=4, replica_groups=mesh['exp'=64,'sub'=4] {'exp'}, use_global_device_ids=true, to_apply=%region_3.4.clone | all-reduce | flops 512 | bytes 4096
  389.8 0.7 fusion.81
  390.5 1.4 fusion.86
  392.0 77.8 %all-gather.6.cloned.1.call-done = bf16[512,1024]{1,0:T(8,128)(2,1)} async-done(((bf16[8,1024]{1,0:T(8,128)(2,1)}), bf16[512,1024]{1,0:T(8,128)(2,1)}) %all-gather.6.cloned.1.call-update) | async-done | bytes 1048592 | tf_op jit(solution)/shard_map/all_gather | solution.py:76
  469.8 1.6 fusion.36
  471.4 3.1 collective-permute-start.4
  474.5 1.3 collective-permute-start.5
  475.8 3.3 collective-permute-done.5
  479.2 2.1 convert_bitcast_fusion
  481.3 1.9 fusion.40
  483.2 3.3 fusion.6
  486.6 6.6 copy.100
  493.1 4.1 fusion.2
  497.3 0.1 subtract_clamp_fusion
  497.4 0.8 copy-done.10
  498.2 2.4 fusion.3
  500.6 3.8 reshape.126
  504.4 3.3 fusion.21
  507.7 0.6 slice_bitcast_fusion.3
  508.3 0.4 copy-done.7
  508.7 1.2 fusion.28
  510.0 3.1 collective-permute-start.6
  513.1 1.3 collective-permute-start.7
  514.4 3.7 collective-permute-done.7
  518.1 0.1 fusion.50
  518.2 2.4 fusion.44
  520.6 187.0 %all-reduce.22.cloned.1.call-done = f32[512,1024]{1,0:T(8,128)} async-done(((f32[512,1024]{1,0:T(8,128)}), f32[512,1024]{1,0:T(8,128)}) %all-reduce.22.cloned.1.call-update) | async-done | bytes 2097168
  707.6 0.9 fusion.76
  708.4 0.6 copy.108
  (44 shorter events, 0.5 us)
Async XLA Ops:
  7.2 3.3 copy-start
  7.2 85.1 %all-gather.4.cloned.1.call-start = ((), (), s32[]{:S(2)}) async-start(), calls=%async_computation | async-start | bytes 1064960 | tf_op jit(solution)/shard_map/all_gather | solution.py:76
  8.6 381.8 %all-reduce.20.cloned.1.call-start = ((), (), s32[]{:S(2)}) async-start(), calls=%async_computation.2 | async-start | bytes 4194304
  11.0 91.8 %copy-start.5 = (bf16[128,148,12]{0,2,1:T(8,128)(2,1)}, bf16[128,148,12]{0,2,1:T(8,128)(2,1)S(1)}, u32[]{:S(2)}) copy-start(bf16[128,148,12]{0,2,1:T(8,128)(2,1)S(1)} %fusion.26) | copy-start | bytes 1363972
  94.0 5.6 collective-permute-start
  97.1 4.7 collective-permute-start.1
  99.5 5.1 copy-start.3
  108.0 6.7 copy-start.2
  114.7 4.1 copy-start.8
  131.2 1.1 copy-start.6
  133.5 11.0 %copy-start.12 = (u32[256]{0:T(256)S(1)}, u32[256]{0:T(256)}, u32[]{:S(2)}) copy-start(u32[256]{0:T(256)} %constant.52) | copy-start | bytes 3076
  133.5 256.9 %copy-start.11 = (f32[1,8,8,128]{3,2,1,0:T(8,128)S(1)}, f32[1,8,8,128]{3,2,1,0:T(8,128)}, u32[]{:S(2)}) copy-start(f32[1,8,8,128]{3,2,1,0:T(8,128)} %param.7) | copy-start | bytes 98308
  133.6 4.6 collective-permute-start.2
  136.7 5.0 collective-permute-start.3
  144.2 325.5 %all-gather.6.cloned.1.call-start = ((), (), s32[]{:S(2)}) async-start(), calls=%async_computation.1 | async-start | bytes 1064960 | tf_op jit(solution)/shard_map/all_gather | solution.py:76
  391.9 315.7 %all-reduce.22.cloned.1.call-start = ((), (), s32[]{:S(2)}) async-start(), calls=%async_computation.3 | async-start | bytes 4194304
  471.4 4.4 collective-permute-start.4
  474.5 4.7 collective-permute-start.5
  481.3 1.9 copy-start.4
  493.1 4.1 copy-start.9
  497.4 0.8 copy-start.10
  507.7 1.1 copy-start.7
  508.7 200.3 %copy-start.1 = (bf16[12,21]{1,0:T(8,128)(2,1)S(1)}, bf16[12,21]{1,0:T(8,128)(2,1)}, u32[]{:S(2)}) copy-start(bf16[12,21]{1,0:T(8,128)(2,1)} %param.10) | copy-start | bytes 1516
  510.0 4.5 collective-permute-start.6
  513.1 5.0 collective-permute-start.7
Sparse Core Ops, SparseCore 0:
  11.3 80.9 all-gather.3
  144.3 187.3 all-reduce.19
  392.0 77.6 all-gather.5
  520.7 186.8 all-reduce.21
where the time goes:
time: 718 us; the launch traced here: 716 us
  waiting for transfers between devices  359 us (50%)
  blocking collectives  244 us (34%)
  local copies, waits for them, and re-layouts  32.5 us (5%)
  matrix products  29.4 us (4%)
  starting transfers between devices  18 us (3%)
  other arithmetic  18 us (3%)
  between operations  14.9 us (2%)
    unnamed x1, blocking collectives  244 us
    unnamed x6, waiting for transfers between devices  187 us
    all_gather x2, waiting for transfers between devices, per_device(): lax.all_gather(current.astype(jnp.bfloat16).reshape(1, per_tile, patch_si...  159 us
  transfers between devices with their start and end apart: 12, of which 7 were waited for; matrix products, arithmetic and copies ran while one was open for 1% of the time, Pallas kernels for 0%

commit v1 on v0

v1 whole, which is shorter than its diff:
```python
import jax
import jax.numpy as jnp
from jax import lax
from jax.experimental import pallas as pl
from jax.experimental.pallas import tpu as pltpu
from jax.sharding import PartitionSpec as P

ETA = 0.5
DELTA = 1.0

NZ, NX, NC = 8, 4, 2
COLS = NX * NC
MODES = 12
TAPS = 21
MARGIN = 10
PIECES = 2
HEIGHT = 128
BREADTH = 512
HALO = 16
EXT = HEIGHT + 2 * HALO
PER_TILE = 8
PH = 8
PW = 128
ROWS = HEIGHT // PH
QCOLS = BREADTH // PW
SIZE = PH * PW
WIDE = SIZE + PW
NEAR_ORDER = (0, 1, 7, 2, 6, 3, 5, 4)
FAR_ORDER = (4, 3, 5, 2, 6, 1, 7)
VMEM_LIMIT = 60 * 1024 * 1024


def place():
    e = lax.axis_index("exp")
    y = lax.axis_index("sub")
    return e // COLS, lax.rem(e // NC, NX), lax.rem(e, NC), y


def at_exp(z, x, c):
    return {"exp": (z * NX + x) * NC + c}


def remote(src, dst, send_sem, recv_sem, device):
    return pltpu.make_async_remote_copy(
        src_ref=src, dst_ref=dst, send_sem=send_sem, recv_sem=recv_sem,
        device_id=device, device_id_type=pl.DeviceIdType.MESH,
    )


def greet(across):
    z, x, c, y = place()
    barrier = pltpu.get_barrier_semaphore()
    many = 0
    for dz in range(1, NZ):
        pl.semaphore_signal(barrier, inc=1, device_id=at_exp(lax.rem(z + dz, NZ), x, c))
        many += 1
    for dx in range(NX):
        for dc in range(NC):
            if dx + dc > 0 and (dc == 0 or dx == 0 or across):
                pl.semaphore_signal(
                    barrier, inc=1, device_id=at_exp(z, lax.rem(x + dx, NX), lax.rem(c + dc, NC))
                )
                many += 1
    bands = lax.axis_size("sub")

    @pl.when(y > 0)
    def _():
        pl.semaphore_signal(barrier, inc=1, device_id={"sub": y - 1})

    @pl.when(y < bands - 1)
    def _():
        pl.semaphore_signal(barrier, inc=1, device_id={"sub": y + 1})

    pl.semaphore_wait(barrier, many + jnp.minimum(y, 1) + jnp.minimum(bands - 1 - y, 1))


def spread_tiles(table, sems):
    (zs, zr, xs, xr, cs, cr) = sems
    z, x, c, _ = place()
    col = x * NC + c

    def tile(col_at, z_at):
        return table.at[pl.ds((col_at * NZ + z_at) * PER_TILE, PER_TILE)]

    def along_z(dz, back):
        z_from = lax.rem(z - dz + NZ, NZ) if back else z
        block = tile(col, z_from)
        return remote(block, block, zs.at[dz], zr.at[dz], at_exp(lax.rem(z + dz, NZ), x, c))

    def along_x(dz, dx, back):
        x_from = lax.rem(x - dx + NX, NX) if back else x
        block = tile(x_from * NC + c, lax.rem(z - dz + NZ, NZ))
        return remote(block, block, xs.at[dz, dx], xr.at[dz, dx], at_exp(z, lax.rem(x + dx, NX), c))

    def to_twin(dz, dx, back):
        c_from = 1 - c if back else c
        block = tile(lax.rem(x - dx + NX, NX) * NC + c_from, lax.rem(z - dz + NZ, NZ))
        return remote(block, block, cs.at[dz, dx], cr.at[dz, dx], at_exp(z, x, 1 - c))

    for dz in FAR_ORDER:
        along_z(dz, False).start()
    for dz in NEAR_ORDER:
        if dz > 0:
            along_z(dz, True).wait_recv()
        for dx in (2, 1, 3):
            along_x(dz, dx, False).start()
        to_twin(dz, 0, False).start()
    for dz in NEAR_ORDER:
        for dx in (1, 3, 2):
            along_x(dz, dx, True).wait_recv()
            to_twin(dz, dx, False).start()
    for dz in NEAR_ORDER:
        for dx in range(NX):
            to_twin(dz, dx, True).wait_recv()
    for dz in range(NZ):
        if dz > 0:
            along_z(dz, False).wait_send()
        for dx in range(NX):
            if dx > 0:
                along_x(dz, dx, False).wait_send()
            to_twin(dz, dx, False).wait_send()


def gather_rows(wanted, table, ext, pair):
    for p in range(PIECES):
        for q in range(QCOLS):
            both = []
            for half in range(2):
                n = wanted[(p * ROWS + pair * 2 + half) * QCOLS + q]
                both.append(table[n].astype(jnp.float32))
            block = jnp.concatenate(both, axis=0).astype(jnp.bfloat16)
            if isinstance(pair, int):
                start = HALO + pair * 2 * PH
            else:
                start = pl.multiple_of(HALO + pair * 2 * PH, 2 * PH)
            ext[p, pl.ds(start, 2 * PH), q * PW:(q + 1) * PW] = block


def fetch_image(wanted, table, ext, rim_out, rim_in, hs, hr):
    _, _, _, y = place()
    bands = lax.axis_size("sub")
    pairs = ROWS // 2
    gather_rows(wanted, table, ext, 0)
    gather_rows(wanted, table, ext, pairs - 1)
    rim_out[0] = ext[:, HALO:2 * HALO, :]
    rim_out[1] = ext[:, HEIGHT:HEIGHT + HALO, :]
    up = remote(rim_out.at[0], rim_in.at[1], hs.at[0], hr.at[1], {"sub": y - 1})
    down = remote(rim_out.at[1], rim_in.at[0], hs.at[1], hr.at[0], {"sub": y + 1})

    @pl.when(y > 0)
    def _():
        up.start()

    @pl.when(y < bands - 1)
    def _():
        down.start()

    def more(pair, carry):
        gather_rows(wanted, table, ext, pair)
        return carry

    lax.fori_loop(1, pairs - 1, more, 0)
    none = jnp.zeros((PIECES, HALO, BREADTH), jnp.bfloat16)

    @pl.when(y > 0)
    def _():
        down.wait_recv()
        ext[:, 0:HALO, :] = rim_in[0]

    @pl.when(y == 0)
    def _():
        ext[:, 0:HALO, :] = none

    @pl.when(y < bands - 1)
    def _():
        up.wait_recv()
        ext[:, HALO + HEIGHT:EXT, :] = rim_in[1]

    @pl.when(y == bands - 1)
    def _():
        ext[:, HALO + HEIGHT:EXT, :] = none

    @pl.when(y > 0)
    def _():
        up.wait_send()

    @pl.when(y < bands - 1)
    def _():
        down.wait_send()


def reduce_patches(rows, select, extra, sky, sky_new, scratch):
    (rim_in, grad, stacked, outgoing, incoming, line_out, line_in, hs, hr, axs, axr, bzs, bzr) = scratch
    z, x, c, y = place()
    bands = lax.axis_size("sub")
    col = x * NC + c
    up = remote(rows.at[:, pl.ds(0, HALO), :], rim_in.at[1], hs.at[0], hr.at[1], {"sub": y - 1})
    down = remote(
        rows.at[:, pl.ds(HALO + HEIGHT, HALO), :], rim_in.at[0], hs.at[1], hr.at[0], {"sub": y + 1}
    )

    @pl.when(y > 0)
    def _():
        up.start()

    @pl.when(y < bands - 1)
    def _():
        down.start()

    strips = [(p, q, (p * QCOLS + q) * HEIGHT) for p in range(PIECES) for q in range(QCOLS)]
    for p, q, at in strips:
        grad[at:at + HEIGHT, :] = rows[p, HALO:HALO + HEIGHT, q * PW:(q + 1) * PW]

    @pl.when(y > 0)
    def _():
        down.wait_recv()
        for p, q, at in strips:
            grad[at:at + HALO, :] += rim_in[0, p, :, q * PW:(q + 1) * PW]

    @pl.when(y < bands - 1)
    def _():
        up.wait_recv()
        for p, q, at in strips:
            grad[at + HEIGHT - HALO:at + HEIGHT, :] += rim_in[1, p, :, q * PW:(q + 1) * PW]

    for p, q, at in strips:
        for i in range(PH):
            lines = grad[pl.ds(at + i, ROWS, stride=PH), :]
            stacked[at // PH:at // PH + ROWS, i * PW:(i + 1) * PW] = lines.astype(jnp.bfloat16)
    stacked[:, SIZE:] = extra[...]

    def across(half, dx, dc, back):
        x_to, c_to = lax.rem(x + dx, NX), lax.rem(c + dc, NC)
        x_from, c_from = lax.rem(x - dx + NX, NX), lax.rem(c + dc, NC)
        source = x_from * NC + c_from if back else col
        return remote(
            outgoing.at[half, x_to * NC + c_to], incoming.at[half, source],
            axs.at[half, dx, dc], axr.at[half, dx, dc], at_exp(z, x_to, c_to),
        )

    peers = [(2, 0), (2, 1), (1, 0), (1, 1), (3, 0), (3, 1), (0, 1)]
    for half in range(2):
        picked = jnp.dot(
            select[half], stacked[...], preferred_element_type=jnp.float32
        ).astype(jnp.bfloat16)
        outgoing[half] = picked.reshape(COLS, HALO, WIDE)
        for dx, dc in peers:
            across(half, dx, dc, False).start()
        incoming[half, col] = outgoing[half, col]

    def along_z(rel, start_at):
        return remote(
            line_out.at[rel], line_in.at[rel], bzs.at[rel], bzr.at[rel],
            at_exp(lax.rem(z + rel, NZ), x, c),
        )

    for half in range(2):
        for dx, dc in peers[::-1]:
            across(half, dx, dc, True).wait_recv()
        arrived = incoming[half].reshape(COLS * HALO, WIDE)
        marks = arrived[:, SIZE:].astype(jnp.float32).T[0:4 * PER_TILE].astype(jnp.bfloat16)
        totals = jnp.dot(marks, arrived[:, :SIZE], preferred_element_type=jnp.float32)
        many = jnp.dot(
            marks, jnp.ones((COLS * HALO, PW), jnp.bfloat16), preferred_element_type=jnp.float32
        )
        for pos in (2, 1, 3, 0) if half == 0 else (0, 3, 1, 2):
            rel = (pos + 4 * (1 - half) + NZ - 2) % NZ
            line = slice(pos * PER_TILE, (pos + 1) * PER_TILE)
            line_out[rel, :, 0:SIZE] = totals[line].astype(jnp.bfloat16)
            line_out[rel, :, SIZE:] = many[line].astype(jnp.bfloat16)
            if rel > 0:
                along_z(rel, True).start()
    total = line_out[0].astype(jnp.float32)
    for rel in NEAR_ORDER[1:]:
        along_z(rel, False).wait_recv()
        total = total + line_in[rel].astype(jnp.float32)
    scale = ETA / jnp.maximum(total[:, SIZE:], 1.0)
    for i in range(PH):
        old = sky[pl.ds(i, PER_TILE, stride=PH), :]
        sky_new[pl.ds(i, PER_TILE, stride=PH), :] = old - scale * total[:, i * PW:(i + 1) * PW]
    for half in range(2):
        for dx, dc in peers:
            across(half, dx, dc, False).wait_send()
    for rel in range(1, NZ):
        along_z(rel, False).wait_send()

    @pl.when(y > 0)
    def _():
        up.wait_send()

    @pl.when(y < bands - 1)
    def _():
        down.wait_send()


def own_tile(sky, table):
    z, x, c, _ = place()
    start = ((x * NC + c) * NZ + z) * PER_TILE
    for k in range(PER_TILE):
        table[start + k] = sky[k * PH:(k + 1) * PH, :].astype(jnp.bfloat16)


def fetch_scratch():
    return [
        pltpu.VMEM((COLS * NZ * PER_TILE, PH, PW), jnp.bfloat16),
        pltpu.VMEM((2, PIECES, HALO, BREADTH), jnp.bfloat16),
        pltpu.VMEM((2, PIECES, HALO, BREADTH), jnp.bfloat16),
        pltpu.SemaphoreType.DMA((NZ,)),
        pltpu.SemaphoreType.DMA((NZ,)),
        pltpu.SemaphoreType.DMA((NZ, NX)),
        pltpu.SemaphoreType.DMA((NZ, NX)),
        pltpu.SemaphoreType.DMA((NZ, NX)),
        pltpu.SemaphoreType.DMA((NZ, NX)),
        pltpu.SemaphoreType.DMA((2,)),
        pltpu.SemaphoreType.DMA((2,)),
    ]


def reduce_scratch():
    return [
        pltpu.VMEM((2, PIECES, HALO, BREADTH), jnp.float32),
        pltpu.VMEM((PIECES * QCOLS * HEIGHT, PW), jnp.float32),
        pltpu.VMEM((PIECES * ROWS * QCOLS, WIDE), jnp.bfloat16),
        pltpu.VMEM((2, COLS, HALO, WIDE), jnp.bfloat16),
        pltpu.VMEM((2, COLS, HALO, WIDE), jnp.bfloat16),
        pltpu.VMEM((NZ, PER_TILE, WIDE), jnp.bfloat16),
        pltpu.VMEM((NZ, PER_TILE, WIDE), jnp.bfloat16),
        pltpu.SemaphoreType.DMA((2,)),
        pltpu.SemaphoreType.DMA((2,)),
        pltpu.SemaphoreType.DMA((2, NX, NC)),
        pltpu.SemaphoreType.DMA((2, NX, NC)),
        pltpu.SemaphoreType.DMA((NZ,)),
        pltpu.SemaphoreType.DMA((NZ,)),
    ]


N_FETCH = 11
N_REDUCE = 13


def first_kernel(wanted, sky, ext, *scratch):
    table, rim_out, rim_in = scratch[:3]
    greet(False)
    own_tile(sky, table)
    spread_tiles(table, scratch[3:9])
    fetch_image(wanted, table, ext, rim_out, rim_in, *scratch[9:11])


def middle_kernel(wanted, sky, rows, select, extra, sky_new, ext, *scratch):
    table, rim_out, rim_in = scratch[:3]
    greet(True)
    reduce_patches(rows, select, extra, sky, sky_new, scratch[N_FETCH:])
    own_tile(sky_new, table)
    spread_tiles(table, scratch[3:9])
    fetch_image(wanted, table, ext, rim_out, rim_in, *scratch[9:11])


def last_kernel(sky, rows, select, extra, sky_new, *scratch):
    greet(True)
    reduce_patches(rows, select, extra, sky, sky_new, scratch)


def convolve(block, centre, edge, transposed):
    dims = (((1,), (1 if transposed else 0,)), ((), ()))
    half = BREADTH // 2

    def product(a, b):
        return lax.dot_general(a, b, dims, preferred_element_type=jnp.float32)

    left = product(block[:, :half], centre)
    right = product(block[:, half:], centre)
    seam = product(block[:, PW:PW + half], edge)
    return [left[:, :PW], left[:, PW:] + seam[:, :PW], right[:, :PW] + seam[:, PW:], right[:, PW:]]


def compute_kernel(ext, coeffs, observed, tall, wide, bands, seams, clipped, rows, smooth, back, model):
    for p in range(PIECES):
        for m in range(MODES):
            smooth[m, p * HEIGHT:(p + 1) * HEIGHT, :] = jnp.dot(
                tall[m * HEIGHT:(m + 1) * HEIGHT, :], ext[p], preferred_element_type=jnp.float32
            ).astype(jnp.bfloat16)
    model[...] = -observed[...]

    def forward(m, carry):
        parts = convolve(smooth[m], bands[m], seams[m], False)
        for q in range(QCOLS):
            cols = slice(q * PW, (q + 1) * PW)
            for p in range(PIECES):
                model[p, :, cols] += (
                    coeffs[p, m, :, cols].astype(jnp.float32) * parts[q][p * HEIGHT:(p + 1) * HEIGHT]
                )
        return carry

    lax.fori_loop(0, MODES, forward, 0)
    clipped[...] = jnp.clip(model[...], -DELTA, DELTA)

    def adjoint(m, carry):
        weighted = jnp.concatenate(
            [
                (coeffs[p, m].astype(jnp.float32) * clipped[p]).astype(jnp.bfloat16)
                for p in range(PIECES)
            ],
            axis=0,
        )
        parts = convolve(weighted, bands[m], seams[m], True)
        start = pl.multiple_of(m * HEIGHT, HEIGHT)
        for q in range(QCOLS):
            cols = slice(q * PW, (q + 1) * PW)
            for p in range(PIECES):
                back[p, pl.ds(start, HEIGHT), cols] = parts[q][p * HEIGHT:(p + 1) * HEIGHT].astype(
                    jnp.bfloat16
                )
        return carry

    lax.fori_loop(0, MODES, adjoint, 0)
    for p in range(PIECES):
        rows[p] = jnp.dot(wide[...], back[p], preferred_element_type=jnp.float32)


def whole(count, smem=()):
    return [
        pl.BlockSpec(memory_space=pltpu.SMEM if i in smem else pltpu.VMEM) for i in range(count)
    ]


def call(kernel, outs, scratch, smem, collective, *args):
    params = dict(vmem_limit_bytes=VMEM_LIMIT)
    if collective is not None:
        params.update(collective_id=collective, has_side_effects=True)
    return pl.pallas_call(
        kernel,
        out_shape=outs,
        in_specs=whole(len(args), smem),
        out_specs=jax.tree.map(lambda _: pl.BlockSpec(memory_space=pltpu.VMEM), outs),
        scratch_shapes=scratch,
        compiler_params=pltpu.CompilerParams(**params),
    )(*args)


def lag_table(filters, shape, lag):
    lags = lax.broadcasted_iota(jnp.int32, (TAPS,) + shape, 0)
    chosen = (lags == lag[None]).astype(jnp.bfloat16)
    return jnp.tensordot(filters, chosen, axes=1, preferred_element_type=jnp.float32).astype(jnp.bfloat16)


def per_device(sky_map, coeffs, observed, vert_taps, horiz_taps, owner_ids, offset):
    z = lax.axis_index("exp") // COLS
    sky = sky_map.reshape(PER_TILE * PH, PW)

    owner = owner_ids[..., 0]
    col, tile_z = owner % COLS, owner // COLS
    wanted = ((col * NZ + tile_z) * PER_TILE + offset).reshape(-1)

    ranked = owner.transpose(0, 2, 1).reshape(PIECES, QCOLS * ROWS)
    places = jnp.arange(QCOLS * ROWS)
    earlier = (ranked[:, :, None] == ranked[:, None, :]) & (places[None, :] < places[:, None])[None]
    rank = jnp.sum(earlier.astype(jnp.int32), axis=2)
    turned = (ranked // COLS - z + NZ + 2) % NZ
    half, pos = 1 - turned // 4, turned % 4
    piece = jnp.arange(PIECES)[:, None]
    slot = ((half * COLS + ranked % COLS) * 4 + pos) * 4 + piece * 2 + rank
    slots = 2 * COLS * HALO
    select = (
        lax.broadcasted_iota(jnp.int32, (slots, 1), 0) == slot.reshape(1, -1)
    ).astype(jnp.bfloat16).reshape(2, COLS * HALO, PIECES * QCOLS * ROWS)
    mark = pos * PER_TILE + offset.transpose(0, 2, 1).reshape(PIECES, QCOLS * ROWS)
    extra = (mark.reshape(-1, 1) == lax.broadcasted_iota(jnp.int32, (1, PW), 1)).astype(jnp.bfloat16)

    i = lax.broadcasted_iota(jnp.int32, (HEIGHT, EXT), 0)
    a = lax.broadcasted_iota(jnp.int32, (HEIGHT, EXT), 1)
    tall = lag_table(vert_taps, (HEIGHT, EXT), a - HALO - i + MARGIN).reshape(MODES * HEIGHT, EXT)
    wide = tall.T
    side = BREADTH // 2
    w = lax.broadcasted_iota(jnp.int32, (side, side), 0)
    j = lax.broadcasted_iota(jnp.int32, (side, side), 1)
    bands = lag_table(horiz_taps, (side, side), w - j + MARGIN)
    seams = jnp.where((w < PW) != (j < PW), bands, jnp.zeros((), jnp.bfloat16))

    sky_shape = jax.ShapeDtypeStruct(sky.shape, jnp.float32)
    ext_shape = jax.ShapeDtypeStruct((PIECES, EXT, BREADTH), jnp.bfloat16)
    clip_shape = jax.ShapeDtypeStruct(observed.shape, jnp.float32)
    rows_shape = jax.ShapeDtypeStruct((PIECES, EXT, BREADTH), jnp.float32)
    compute_scratch = [
        pltpu.VMEM((MODES, PIECES * HEIGHT, BREADTH), jnp.bfloat16),
        pltpu.VMEM((PIECES, MODES * HEIGHT, BREADTH), jnp.bfloat16),
        pltpu.VMEM((PIECES, HEIGHT, BREADTH), jnp.float32),
    ]

    def compute(ext):
        return call(
            compute_kernel, (clip_shape, rows_shape), compute_scratch, (), None,
            ext, coeffs, observed, tall, wide, bands, seams,
        )

    ext = call(first_kernel, ext_shape, fetch_scratch(), (0,), 0, wanted, sky)
    _, rows = compute(ext)
    sky, ext = call(
        middle_kernel, (sky_shape, ext_shape), fetch_scratch() + reduce_scratch(), (0,), 1,
        wanted, sky, rows, select, extra,
    )
    clipped, rows = compute(ext)
    sky = call(last_kernel, sky_shape, reduce_scratch(), (), 2, sky, rows, select, extra)
    return sky.reshape(sky_map.shape), clipped


def solution(mesh):
    return jax.shard_map(
        per_device,
        mesh=mesh,
        in_specs=(
            P(("exp", "sub"), None, None, None),
            P("exp", None, "sub", None),
            P("exp", "sub", None),
            P(),
            P(),
            P("exp", "sub", None, None),
            P("exp", "sub", None),
        ),
        out_specs=(P(("exp", "sub"), None, None, None), P("exp", "sub", None)),
        check_vma=False,
    )
```

time: 718 us -> 127 us (0.18)
  waiting for transfers between devices: 359 us -> 0 us
  blocking collectives: 244 us -> 0 us
  Pallas kernels: 0 us -> 112 us
  matrix products: 29.4 us -> 1.92 us
  local copies, waits for them, and re-layouts: 32.5 us -> 6.9 us
  starting transfers between devices: 18 us -> 0 us
  between operations: 14.9 us -> 0.78 us
  other arithmetic: 18 us -> 4.59 us
    unnamed x1 -> x0, blocking collectives: 244 us -> none
    unnamed x6 -> x0, waiting for transfers between devices: 187 us -> none
    all_gather x2 -> x0, waiting for transfers between devices: 159 us -> none  [per_device(): lax.all_gather(current.astype(jnp.bfloat16).reshape(1, per_tile, patch_si...]
    pallas_call x0 -> x5, Pallas kernels: none -> 112 us  [call(): pl.pallas_call(kernel, out_shape=outs, in_specs=whole(len(args), smem), o...]
    dot_general x14 -> x2, matrix products: 29.4 us -> 1.92 us  [lag_table(): jnp.tensordot(filters, chosen, axes=1, preferred_element_type=jnp.float32)]
    reshape x6 -> x4, local copies, waits for them, and re-layouts: 22.8 us -> 3.33 us  [the longest x1 1.16 us: per_device(): lag_table(vert_taps, (HEIGHT, EXT), a - HALO - i + MARGIN)]
    ppermute x8 -> x0, starting transfers between devices: 17.8 us -> none  [the longest x4 9.01 us: from_behind(): return lax.ppermute(block, axis, route)]
    ppermute x8 -> x0, waiting for transfers between devices: 12.8 us -> none  [the longest x4 7.23 us: from_behind(): return lax.ppermute(block, axis, route)]
  transfers between devices with their start and end apart: 12 -> 0, of which waited for: 7 -> 0; matrix products, arithmetic and copies ran while one was open for 1% -> 0% of each run, Pallas kernels for 0% -> 0%
where the time goes in v1:
time: 127 us; the launch traced here: 126 us
  Pallas kernels  112 us (88%)
  local copies, waits for them, and re-layouts  6.9 us (5%)
  other arithmetic  4.59 us (4%)
  matrix products  1.92 us (2%)
    pallas_call x5, Pallas kernels, call(): pl.pallas_call(kernel, out_shape=outs, in_specs=whole(len(args), smem), o...  112 us
    select_n x1, other arithmetic, per_device(): seams = jnp.where((w < PW) != (j < PW), bands, jnp.zeros((), jnp.bfloat16))  2.67 us

profile of v1, /device:TPU:1, one launch (start us, length us, event | category | flops | bytes accessed | tf_op | source)
XLA Modules:
  0.0 126.2 jit_solution(6097545174185281609)
XLA Ops:
  0.6 0.0 copy-start
  0.7 0.8 reshape.255
  1.4 0.8 reshape.256
  2.2 0.8 eq.78
  3.0 0.2 convert_reduce_fusion
  3.2 0.1 reduce_sum.12
  3.3 0.1 add.161
  3.4 0.1 add.162
  3.5 0.7 compare_convert_fusion.select
  4.2 0.7 fusion.6.extra
  4.9 0.0 copy-done
  5.0 1.4 %fusion = bf16[256,256,12]{1,2,0:T(8,128)(2,1)S(1)} fusion(s32[256,256]{1,0:T(8,128)S(1)} %subtract_add_fusion, bf16[12,21]{1,0:T(8,128)(2,1)S(1)} %copy-done), kind=kOutput, calls=%fused_computation.1 | convolution fusion | flops 34406400 | bytes 1835512 | tf_op jit(solution)/shard_map/dot_general | solution.py:443
  6.4 0.1 broadcast_compare_fusion
  6.5 0.0 copy-start.3
  6.5 2.7 %broadcast_select_fusion = (bf16[12,256,256]{2,1,0:T(8,128)(2,1)}, bf16[12,256,256]{2,1,0:T(8,128)(2,1)}) fusion(pred[256,256]{1,0:T(8,128)(4,1)S(1)} %broadcast_compare_fusion, bf16[256,256,12]{1,2,0:T(8,128)(2,1)S(1)} %fusion), kind=kLoop, calls=%fused_computation.7 | loop fusion | flops 786432 | bytes 4784128 | tf_op jit(solution)/shard_map/jit(_where)/select_n | solution.py:477
  9.2 0.1 subtract_add_fusion.1
  9.3 0.0 copy-done.3
  9.3 0.5 fusion.4
  9.8 0.0 copy-start.1
  9.8 0.0 copy-start.2
  9.8 0.1 copy.29
  10.0 1.2 copy.19.tall
  11.1 0.9 copy.30
  12.1 0.0 copy-done.1
  12.1 0.0 copy-done.2
  12.1 0.1 copy.17
  12.2 0.6 reshape.252.wanted
  12.8 26.3 %shard_map.86.ext = bf16[2,160,512]{2,1,0:T(8,128)(2,1)} custom-call(s32[128]{0:T(128)} %reshape.252.wanted, f32[64,128]{1,0:T(8,128)} %bitcast.34), custom_call_target="tpu_custom_call" | custom-call | tf_op jit(solution)/shard_map/pallas_call | solution.py:430
  39.1 13.0 %shard_map.87 = (f32[2,128,512]{2,1,0:T(8,128)}, f32[2,160,512]{2,1,0:T(8,128)}) custom-call(bf16[2,160,512]{2,1,0:T(8,128)(2,1)} %shard_map.86.ext, bf16[2,12,128,512]{3,2,1,0:T(8,128)(2,1)} %coeffs.3, f32[2,128,512]{2,1,0:T(8,128)} %observed.3, bf16[1536,160]{1,0:T(8,128)(2,1)} %copy.19.tall, bf16[160,1536]{1,0:T(8,128)(2,1)} %bitcast.30, ...), custom_call_target="tpu_custom_call" | custom-call | tf_op jit(solution)/shard_map/pallas_call | solution.py:430
  52.1 39.7 %shard_map.88 = (f32[64,128]{1,0:T(8,128)}, bf16[2,160,512]{2,1,0:T(8,128)(2,1)}) custom-call(s32[128]{0:T(128)} %reshape.252.wanted, f32[64,128]{1,0:T(8,128)} %bitcast.35, f32[2,160,512]{2,1,0:T(8,128)} %get-tuple-element.7.rows, bf16[2,128,128]{2,1,0:T(8,128)(2,1)} %compare_convert_fusion.select, bf16[128,128]{1,0:T(8,128)(2,1)} %fusion.6.extra), custom_call_target="tpu_custom_call" | custom-call | tf_op jit(solution)/shard_map/pallas_call | solution.py:430
  91.9 13.0 %shard_map.89 = (f32[2,128,512]{2,1,0:T(8,128)}, f32[2,160,512]{2,1,0:T(8,128)}) custom-call(bf16[2,160,512]{2,1,0:T(8,128)(2,1)} %get-tuple-element.9.ext, bf16[2,12,128,512]{3,2,1,0:T(8,128)(2,1)} %coeffs.3, f32[2,128,512]{2,1,0:T(8,128)} %observed.3, bf16[1536,160]{1,0:T(8,128)(2,1)} %copy.19.tall, bf16[160,1536]{1,0:T(8,128)(2,1)} %bitcast.31, ...), custom_call_target="tpu_custom_call" | custom-call | tf_op jit(solution)/shard_map/pallas_call | solution.py:430
  104.8 20.0 %shard_map.90 = f32[64,128]{1,0:T(8,128)} custom-call(f32[64,128]{1,0:T(8,128)} %get-tuple-element.8.sky, f32[2,160,512]{2,1,0:T(8,128)} %get-tuple-element.10.rows, bf16[2,128,128]{2,1,0:T(8,128)(2,1)} %compare_convert_fusion.select, bf16[128,128]{1,0:T(8,128)(2,1)} %fusion.6.extra), custom_call_target="tpu_custom_call" | custom-call | tf_op jit(solution)/shard_map/pallas_call | solution.py:430
  124.8 1.4 %copy.32 = f32[1,8,8,128]{3,2,1,0:T(8,128)} copy(f32[1,8,8,128]{3,2,1,0:T(8,128)} %bitcast.33) | data formatting | bytes 65536
  (9 shorter events, 0.1 us)
Async XLA Ops:
  0.6 4.3 %copy-start = (bf16[12,21]{1,0:T(8,128)(2,1)S(1)}, bf16[12,21]{1,0:T(8,128)(2,1)}, u32[]{:S(2)}) copy-start(bf16[12,21]{1,0:T(8,128)(2,1)} %param.11) | copy-start | bytes 1516
  6.5 2.8 %copy-start.3 = (bf16[12,21]{1,0:T(8,128)(2,1)S(1)}, bf16[12,21]{1,0:T(8,128)(2,1)}, u32[]{:S(2)}) copy-start(bf16[12,21]{1,0:T(8,128)(2,1)} %param.10) | copy-start | bytes 1516
  9.8 2.3 %copy-start.1 = (s32[2,16,4,1]{1,3,2,0:T(1,128)S(1)}, s32[2,16,4,1]{1,3,2,0:T(1,128)}, u32[]{:S(2)}) copy-start(s32[2,16,4,1]{1,3,2,0:T(1,128)} %param.12) | copy-start | bytes 1540
  9.8 2.2 %copy-start.2 = (s32[2,16,4]{1,2,0:T(4,128)S(1)}, s32[2,16,4]{1,2,0:T(4,128)}, u32[]{:S(2)}) copy-start(s32[2,16,4]{1,2,0:T(4,128)} %param.13) | copy-start | bytes 1540

commit v2 on v1

--- a/solution.py
+++ b/solution.py
@@ -5,6 +5,7 @@
 from jax.experimental.pallas import tpu as pltpu
 from jax.sharding import PartitionSpec as P
 
+STEPS = 2
 ETA = 0.5
 DELTA = 1.0
 
@@ -47,7 +48,7 @@
     )
 
 
-def greet(across):
+def greet():
     z, x, c, y = place()
     barrier = pltpu.get_barrier_semaphore()
     many = 0
@@ -56,7 +57,7 @@
         many += 1
     for dx in range(NX):
         for dc in range(NC):
-            if dx + dc > 0 and (dc == 0 or dx == 0 or across):
+            if dx + dc > 0:
                 pl.semaphore_signal(
                     barrier, inc=1, device_id=at_exp(z, lax.rem(x + dx, NX), lax.rem(c + dc, NC))
                 )
@@ -71,10 +72,12 @@
     def _():
         pl.semaphore_signal(barrier, inc=1, device_id={"sub": y + 1})
 
-    pl.semaphore_wait(barrier, many + jnp.minimum(y, 1) + jnp.minimum(bands - 1 - y, 1))
-
-
-def spread_tiles(table, sems):
+    return lambda: pl.semaphore_wait(
+        barrier, many + jnp.minimum(y, 1) + jnp.minimum(bands - 1 - y, 1)
+    )
+
+
+def spread_tiles(table, sems, early, late):
     (zs, zr, xs, xr, cs, cr) = sems
     z, x, c, _ = place()
     col = x * NC + c
@@ -99,12 +102,14 @@
 
     for dz in FAR_ORDER:
         along_z(dz, False).start()
+    early()
     for dz in NEAR_ORDER:
         if dz > 0:
             along_z(dz, True).wait_recv()
         for dx in (2, 1, 3):
             along_x(dz, dx, False).start()
         to_twin(dz, 0, False).start()
+    late()
     for dz in NEAR_ORDER:
         for dx in (1, 3, 2):
             along_x(dz, dx, True).wait_recv()
@@ -121,13 +126,15 @@
             to_twin(dz, dx, False).wait_send()
 
 
-def gather_rows(wanted, table, ext, pair):
+def gather_rows(owners, offsets, table, ext, pair):
     for p in range(PIECES):
         for q in range(QCOLS):
             both = []
             for half in range(2):
-                n = wanted[(p * ROWS + pair * 2 + half) * QCOLS + q]
-                both.append(table[n].astype(jnp.float32))
+                r = pair * 2 + half
+                owner = owners[p, q, 0, r]
+                tile = lax.rem(owner, COLS) * NZ + owner // COLS
+                both.append(table[tile * PER_TILE + offsets[p, q, r]].astype(jnp.float32))
             block = jnp.concatenate(both, axis=0).astype(jnp.bfloat16)
             if isinstance(pair, int):
                 start = HALO + pair * 2 * PH
@@ -136,12 +143,12 @@
             ext[p, pl.ds(start, 2 * PH), q * PW:(q + 1) * PW] = block
 
 
-def fetch_image(wanted, table, ext, rim_out, rim_in, hs, hr):
+def fetch_image(owners, offsets, table, ext, rim_out, rim_in, hs, hr):
     _, _, _, y = place()
     bands = lax.axis_size("sub")
     pairs = ROWS // 2
-    gather_rows(wanted, table, ext, 0)
-    gather_rows(wanted, table, ext, pairs - 1)
+    gather_rows(owners, offsets, table, ext, 0)
+    gather_rows(owners, offsets, table, ext, pairs - 1)
     rim_out[0] = ext[:, HALO:2 * HALO, :]
     rim_out[1] = ext[:, HEIGHT:HEIGHT + HALO, :]
     up = remote(rim_out.at[0], rim_in.at[1], hs.at[0], hr.at[1], {"sub": y - 1})
@@ -156,7 +163,7 @@
         down.start()
 
     def more(pair, carry):
-        gather_rows(wanted, table, ext, pair)
+        gather_rows(owners, offsets, table, ext, pair)
         return carry
 
     lax.fori_loop(1, pairs - 1, more, 0)
@@ -190,7 +197,8 @@
 
 
 def reduce_patches(rows, select, extra, sky, sky_new, scratch):
-    (rim_in, grad, stacked, outgoing, incoming, line_out, line_in, hs, hr, axs, axr, bzs, bzr) = scratch
+    (rim_in, grad, stacked, outgoing, incoming, line_out, line_in), sems = scratch
+    hs, hr, axs, axr, bzs, bzr = sems
     z, x, c, y = place()
     bands = lax.axis_size("sub")
     col = x * NC + c
@@ -300,66 +308,6 @@
         table[start + k] = sky[k * PH:(k + 1) * PH, :].astype(jnp.bfloat16)
 
 
-def fetch_scratch():
-    return [
-        pltpu.VMEM((COLS * NZ * PER_TILE, PH, PW), jnp.bfloat16),
-        pltpu.VMEM((2, PIECES, HALO, BREADTH), jnp.bfloat16),
-        pltpu.VMEM((2, PIECES, HALO, BREADTH), jnp.bfloat16),
-        pltpu.SemaphoreType.DMA((NZ,)),
-        pltpu.SemaphoreType.DMA((NZ,)),
-        pltpu.SemaphoreType.DMA((NZ, NX)),
-        pltpu.SemaphoreType.DMA((NZ, NX)),
-        pltpu.SemaphoreType.DMA((NZ, NX)),
-        pltpu.SemaphoreType.DMA((NZ, NX)),
-        pltpu.SemaphoreType.DMA((2,)),
-        pltpu.SemaphoreType.DMA((2,)),
-    ]
-
-
-def reduce_scratch():
-    return [
-        pltpu.VMEM((2, PIECES, HALO, BREADTH), jnp.float32),
-        pltpu.VMEM((PIECES * QCOLS * HEIGHT, PW), jnp.float32),
-        pltpu.VMEM((PIECES * ROWS * QCOLS, WIDE), jnp.bfloat16),
-        pltpu.VMEM((2, COLS, HALO, WIDE), jnp.bfloat16),
-        pltpu.VMEM((2, COLS, HALO, WIDE), jnp.bfloat16),
-        pltpu.VMEM((NZ, PER_TILE, WIDE), jnp.bfloat16),
-        pltpu.VMEM((NZ, PER_TILE, WIDE), jnp.bfloat16),
-        pltpu.SemaphoreType.DMA((2,)),
-        pltpu.SemaphoreType.DMA((2,)),
-        pltpu.SemaphoreType.DMA((2, NX, NC)),
-        pltpu.SemaphoreType.DMA((2, NX, NC)),
-        pltpu.SemaphoreType.DMA((NZ,)),
-        pltpu.SemaphoreType.DMA((NZ,)),
-    ]
-
-
-N_FETCH = 11
-N_REDUCE = 13
-
-
-def first_kernel(wanted, sky, ext, *scratch):
-    table, rim_out, rim_in = scratch[:3]
-    greet(False)
-    own_tile(sky, table)
-    spread_tiles(table, scratch[3:9])
-    fetch_image(wanted, table, ext, rim_out, rim_in, *scratch[9:11])
-
-
-def middle_kernel(wanted, sky, rows, select, extra, sky_new, ext, *scratch):
-    table, rim_out, rim_in = scratch[:3]
-    greet(True)
-    reduce_patches(rows, select, extra, sky, sky_new, scratch[N_FETCH:])
-    own_tile(sky_new, table)
-    spread_tiles(table, scratch[3:9])
-    fetch_image(wanted, table, ext, rim_out, rim_in, *scratch[9:11])
-
-
-def last_kernel(sky, rows, select, extra, sky_new, *scratch):
-    greet(True)
-    reduce_patches(rows, select, extra, sky, sky_new, scratch)
-
-
 def convolve(block, centre, edge, transposed):
     dims = (((1,), (1 if transposed else 0,)), ((), ()))
     half = BREADTH // 2
@@ -373,7 +321,98 @@
     return [left[:, :PW], left[:, PW:] + seam[:, :PW], right[:, :PW] + seam[:, PW:], right[:, PW:]]
 
 
-def compute_kernel(ext, coeffs, observed, tall, wide, bands, seams, clipped, rows, smooth, back, model):
+def diagonals(row, height):
+    return pltpu.roll(jnp.broadcast_to(row, (height, row.shape[1])), 0, 1, stride=1, stride_axis=0)
+
+
+def lag_rows(taps, lag):
+    tap = lax.broadcasted_iota(jnp.int32, (TAPS, 2 * PW), 0)
+    lane = lax.broadcasted_iota(jnp.int32, (TAPS, 2 * PW), 1)
+    chosen = (tap == lag(lane)).astype(jnp.bfloat16)
+    return jnp.dot(taps[...], chosen, preferred_element_type=jnp.float32)
+
+
+def wrapped(lane):
+    return jnp.where(lane < PW, lane, lane - 2 * PW)
+
+
+def build_tall(vert, base, tall):
+    base[...] = lag_rows(vert, lambda lane: lane - HALO + MARGIN)
+
+    def one(m, carry):
+        rows = diagonals(base[pl.ds(m, 1), :], HEIGHT)
+        tall[pl.ds(pl.multiple_of(m * HEIGHT, HEIGHT), HEIGHT), :] = rows[:, :EXT].astype(jnp.bfloat16)
+        return carry
+
+    lax.fori_loop(0, MODES, one, 0)
+
+
+def build_wide(vert, base, wide):
+    base[...] = lag_rows(vert, lambda lane: MARGIN - HALO - wrapped(lane))
+
+    def one(m, carry):
+        rows = diagonals(base[pl.ds(m, 1), :], EXT)
+        wide[m] = rows[:, :HEIGHT].astype(jnp.bfloat16)
+        return carry
+
+    lax.fori_loop(0, MODES, one, 0)
+
+
+def build_bands(horiz, base, bands, seams):
+    base[...] = lag_rows(horiz, lambda lane: MARGIN - wrapped(lane))
+    side = BREADTH // 2
+    w = lax.broadcasted_iota(jnp.int32, (side, side), 0)
+    c = lax.broadcasted_iota(jnp.int32, (side, side), 1)
+    near = jnp.abs(w - c) <= MARGIN
+    across = near & ((w < PW) != (c < PW))
+
+    def one(m, carry):
+        rows = diagonals(base[pl.ds(m, 1), :], side)
+        bands[m] = jnp.where(near, rows, 0.0).astype(jnp.bfloat16)
+        seams[m] = jnp.where(across, rows, 0.0).astype(jnp.bfloat16)
+        return carry
+
+    lax.fori_loop(0, MODES, one, 0)
+
+
+def build_slots(owners, offsets, own_rows, off_rows, select, extra):
+    z, _, _, _ = place()
+
+    def one(r, carry):
+        for p in range(PIECES):
+            for q in range(QCOLS):
+                n = (p * QCOLS + q) * ROWS + r
+                own_rows[pl.ds(n, 1), :] = jnp.full((1, PW), owners[p, q, 0, r], jnp.int32)
+                off_rows[pl.ds(n, 1), :] = jnp.full((1, PW), offsets[p, q, r], jnp.int32)
+        return carry
+
+    lax.fori_loop(0, ROWS, one, 0)
+    count = PIECES * QCOLS * ROWS
+    down = lax.broadcasted_iota(jnp.int32, (count, count), 0)
+    along = lax.broadcasted_iota(jnp.int32, (count, count), 1)
+    per_piece = QCOLS * ROWS
+    own = own_rows[...]
+    own_along = own.T
+    earlier = (own == own_along) & (down < along) & ((down < per_piece) == (along < per_piece))
+    rank = jnp.sum(earlier.astype(jnp.int32), axis=0, keepdims=True)
+    across = own_along[0:1, :]
+
+    def turned(owner):
+        return lax.rem(owner // COLS - z + NZ + 2, NZ)
+
+    spin = turned(across)
+    half, pos = 1 - spin // 4, lax.rem(spin, 4)
+    piece = along[0:1, :] // per_piece
+    slot = ((half * COLS + lax.rem(across, COLS)) * 4 + pos) * 4 + piece * 2 + rank
+    for h in range(2):
+        select[h] = (down + h * count == slot).astype(jnp.bfloat16)
+    mark = lax.rem(turned(own), 4) * PER_TILE + off_rows[...]
+    extra[...] = (mark == along).astype(jnp.bfloat16)
+
+
+def compute(ext, coeffs, observed, tables, clipped, rows, scratch):
+    tall, wide, bands, seams = tables
+    smooth, back, model = scratch
     for p in range(PIECES):
         for m in range(MODES):
             smooth[m, p * HEIGHT:(p + 1) * HEIGHT, :] = jnp.dot(
@@ -413,94 +452,119 @@
         return carry
 
     lax.fori_loop(0, MODES, adjoint, 0)
+    turned = jnp.concatenate([wide[m] for m in range(MODES)], axis=1)
     for p in range(PIECES):
-        rows[p] = jnp.dot(wide[...], back[p], preferred_element_type=jnp.float32)
-
-
-def whole(count, smem=()):
-    return [
-        pl.BlockSpec(memory_space=pltpu.SMEM if i in smem else pltpu.VMEM) for i in range(count)
+        rows[p] = jnp.dot(turned, back[p], preferred_element_type=jnp.float32)
+
+
+def kernel(owners, offsets, sky, coeffs_far, observed_far, vert, horiz, sky_out, clipped, *scratch):
+    (
+        coeffs, observed, base, tall, wide, bands, seams, own_rows, off_rows, select, extra,
+        table, rim_out, rim_in, ext, smooth, back, model, rows, sky_mid, *scratch
+    ) = scratch
+    load, fetch_sems, reduce_refs, reduce_sems = scratch[0], scratch[1:9], scratch[9:16], scratch[16:]
+    loads = [
+        pltpu.make_async_copy(coeffs_far, coeffs, load.at[0]),
+        pltpu.make_async_copy(observed_far, observed, load.at[1]),
     ]
-
-
-def call(kernel, outs, scratch, smem, collective, *args):
-    params = dict(vmem_limit_bytes=VMEM_LIMIT)
-    if collective is not None:
-        params.update(collective_id=collective, has_side_effects=True)
-    return pl.pallas_call(
+    all_here = greet()
+    for copy in loads:
+        copy.start()
+    own_tile(sky, table)
+    build_tall(vert, base, tall)
+    all_here()
+
+    def early():
+        build_wide(vert, base, wide)
+
+    def late():
+        build_bands(horiz, base, bands, seams)
+        build_slots(owners, offsets, own_rows, off_rows, select, extra)
+
+    def nothing():
+        pass
+
+    for step in range(STEPS):
+        first = step == 0
+        sems = [ref.at[step] for ref in fetch_sems]
+        spread_tiles(table, sems[:6], early if first else nothing, late if first else nothing)
+        fetch_image(owners, offsets, table, ext, rim_out, rim_in, *sems[6:])
+        if first:
+            for copy in loads:
+                copy.wait()
+        compute(ext, coeffs, observed, (tall, wide, bands, seams), clipped, rows, (smooth, back, model))
+        sems = [ref.at[step] for ref in reduce_sems]
+        before, after = (sky, sky_mid) if first else (sky_mid, sky_out)
+        reduce_patches(rows, select, extra, before, after, (reduce_refs, sems))
+        if first:
+            own_tile(sky_mid, table)
+
+
+def per_device(sky_map, coeffs, observed, vert_taps, horiz_taps, owner_ids, offset):
+    sky = sky_map.reshape(PER_TILE * PH, PW)
+    bf16, f32, i32 = jnp.bfloat16, jnp.float32, jnp.int32
+    side = BREADTH // 2
+    count = PIECES * QCOLS * ROWS
+    dma = pltpu.SemaphoreType.DMA
+    scratch = [
+        pltpu.VMEM(coeffs.shape, bf16),
+        pltpu.VMEM(observed.shape, f32),
+        pltpu.VMEM((MODES, side), f32),
+        pltpu.VMEM((MODES * HEIGHT, EXT), bf16),
+        pltpu.VMEM((MODES, EXT, HEIGHT), bf16),
+        pltpu.VMEM((MODES, side, side), bf16),
+        pltpu.VMEM((MODES, side, side), bf16),
+        pltpu.VMEM((count, PW), i32),
+        pltpu.VMEM((count, PW), i32),
+        pltpu.VMEM((2, count, count), bf16),
+        pltpu.VMEM((count, PW), bf16),
+        pltpu.VMEM((COLS * NZ * PER_TILE, PH, PW), bf16),
+        pltpu.VMEM((2, PIECES, HALO, BREADTH), bf16),
+        pltpu.VMEM((2, PIECES, HALO, BREADTH), bf16),
+        pltpu.VMEM((PIECES, EXT, BREADTH), bf16),
+        pltpu.VMEM((MODES, PIECES * HEIGHT, BREADTH), bf16),
+        pltpu.VMEM((PIECES, MODES * HEIGHT, BREADTH), bf16),
+        pltpu.VMEM((PIECES, HEIGHT, BREADTH), f32),
+        pltpu.VMEM((PIECES, EXT, BREADTH), f32),
+        pltpu.VMEM((PER_TILE * PH, PW), f32),
+        dma((2,)),
+        dma((STEPS, NZ)),
+        dma((STEPS, NZ)),
+        dma((STEPS, NZ, NX)),
+        dma((STEPS, NZ, NX)),
+        dma((STEPS, NZ, NX)),
+        dma((STEPS, NZ, NX)),
+        dma((STEPS, 2)),
+        dma((STEPS, 2)),
+        pltpu.VMEM((2, PIECES, HALO, BREADTH), f32),
+        pltpu.VMEM((PIECES * QCOLS * HEIGHT, PW), f32),
+        pltpu.VMEM((count, WIDE), bf16),
+        pltpu.VMEM((2, COLS, HALO, WIDE), bf16),
+        pltpu.VMEM((2, COLS, HALO, WIDE), bf16),
+        pltpu.VMEM((NZ, PER_TILE, WIDE), bf16),
+        pltpu.VMEM((NZ, PER_TILE, WIDE), bf16),
+        dma((STEPS, 2)),
+        dma((STEPS, 2)),
+        dma((STEPS, 2, NX, NC)),
+        dma((STEPS, 2, NX, NC)),
+        dma((STEPS, NZ)),
+        dma((STEPS, NZ)),
+    ]
+    smem, vmem, far = pltpu.SMEM, pltpu.VMEM, pl.ANY
+    sky_new, clipped = pl.pallas_call(
         kernel,
-        out_shape=outs,
-        in_specs=whole(len(args), smem),
-        out_specs=jax.tree.map(lambda _: pl.BlockSpec(memory_space=pltpu.VMEM), outs),
+        out_shape=(
+            jax.ShapeDtypeStruct(sky.shape, f32),
+            jax.ShapeDtypeStruct(observed.shape, f32),
+        ),
+        in_specs=[pl.BlockSpec(memory_space=m) for m in (smem, smem, vmem, far, far, vmem, vmem)],
+        out_specs=(pl.BlockSpec(memory_space=vmem), pl.BlockSpec(memory_space=vmem)),
         scratch_shapes=scratch,
-        compiler_params=pltpu.CompilerParams(**params),
-    )(*args)
-
-
-def lag_table(filters, shape, lag):
-    lags = lax.broadcasted_iota(jnp.int32, (TAPS,) + shape, 0)
-    chosen = (lags == lag[None]).astype(jnp.bfloat16)
-    return jnp.tensordot(filters, chosen, axes=1, preferred_element_type=jnp.float32).astype(jnp.bfloat16)
-
-
-def per_device(sky_map, coeffs, observed, vert_taps, horiz_taps, owner_ids, offset):
-    z = lax.axis_index("exp") // COLS
-    sky = sky_map.reshape(PER_TILE * PH, PW)
-
-    owner = owner_ids[..., 0]
-    col, tile_z = owner % COLS, owner // COLS
-    wanted = ((col * NZ + tile_z) * PER_TILE + offset).reshape(-1)
-
-    ranked = owner.transpose(0, 2, 1).reshape(PIECES, QCOLS * ROWS)
-    places = jnp.arange(QCOLS * ROWS)
-    earlier = (ranked[:, :, None] == ranked[:, None, :]) & (places[None, :] < places[:, None])[None]
-    rank = jnp.sum(earlier.astype(jnp.int32), axis=2)
-    turned = (ranked // COLS - z + NZ + 2) % NZ
-    half, pos = 1 - turned // 4, turned % 4
-    piece = jnp.arange(PIECES)[:, None]
-    slot = ((half * COLS + ranked % COLS) * 4 + pos) * 4 + piece * 2 + rank
-    slots = 2 * COLS * HALO
-    select = (
-        lax.broadcasted_iota(jnp.int32, (slots, 1), 0) == slot.reshape(1, -1)
-    ).astype(jnp.bfloat16).reshape(2, COLS * HALO, PIECES * QCOLS * ROWS)
-    mark = pos * PER_TILE + offset.transpose(0, 2, 1).reshape(PIECES, QCOLS * ROWS)
-    extra = (mark.reshape(-1, 1) == lax.broadcasted_iota(jnp.int32, (1, PW), 1)).astype(jnp.bfloat16)
-
-    i = lax.broadcasted_iota(jnp.int32, (HEIGHT, EXT), 0)
-    a = lax.broadcasted_iota(jnp.int32, (HEIGHT, EXT), 1)
-    tall = lag_table(vert_taps, (HEIGHT, EXT), a - HALO - i + MARGIN).reshape(MODES * HEIGHT, EXT)
-    wide = tall.T
-    side = BREADTH // 2
-    w = lax.broadcasted_iota(jnp.int32, (side, side), 0)
-    j = lax.broadcasted_iota(jnp.int32, (side, side), 1)
-    bands = lag_table(horiz_taps, (side, side), w - j + MARGIN)
-    seams = jnp.where((w < PW) != (j < PW), bands, jnp.zeros((), jnp.bfloat16))
-
-    sky_shape = jax.ShapeDtypeStruct(sky.shape, jnp.float32)
-    ext_shape = jax.ShapeDtypeStruct((PIECES, EXT, BREADTH), jnp.bfloat16)
-    clip_shape = jax.ShapeDtypeStruct(observed.shape, jnp.float32)
-    rows_shape = jax.ShapeDtypeStruct((PIECES, EXT, BREADTH), jnp.float32)
-    compute_scratch = [
-        pltpu.VMEM((MODES, PIECES * HEIGHT, BREADTH), jnp.bfloat16),
-        pltpu.VMEM((PIECES, MODES * HEIGHT, BREADTH), jnp.bfloat16),
-        pltpu.VMEM((PIECES, HEIGHT, BREADTH), jnp.float32),
-    ]
-
-    def compute(ext):
-        return call(
-            compute_kernel, (clip_shape, rows_shape), compute_scratch, (), None,
-            ext, coeffs, observed, tall, wide, bands, seams,
-        )
-
-    ext = call(first_kernel, ext_shape, fetch_scratch(), (0,), 0, wanted, sky)
-    _, rows = compute(ext)
-    sky, ext = call(
-        middle_kernel, (sky_shape, ext_shape), fetch_scratch() + reduce_scratch(), (0,), 1,
-        wanted, sky, rows, select, extra,
-    )
-    clipped, rows = compute(ext)
-    sky = call(last_kernel, sky_shape, reduce_scratch(), (), 2, sky, rows, select, extra)
-    return sky.reshape(sky_map.shape), clipped
+        compiler_params=pltpu.CompilerParams(
+            vmem_limit_bytes=VMEM_LIMIT, collective_id=0, has_side_effects=True
+        ),
+    )(owner_ids.transpose(0, 2, 3, 1), offset.transpose(0, 2, 1), sky, coeffs, observed, vert_taps, horiz_taps)
+    return sky_new.reshape(sky_map.shape), clipped
 
 
 def solution(mesh):

time: 127 us -> 99.4 us (0.78)
  Pallas kernels: 112 us -> 95.3 us
  other arithmetic: 4.59 us -> 0 us
  local copies, waits for them, and re-layouts: 6.9 us -> 3.24 us
  matrix products: 1.92 us -> 0 us
    pallas_call x5 -> x1, Pallas kernels: 112 us -> 95.3 us  [per_device(): pl.pallas_call(kernel, out_shape=(jax.ShapeDtypeStruct(sky.shape, f32), j...]
    reshape x4 -> x0, local copies, waits for them, and re-layouts: 3.33 us -> none  [the longest x1 1.16 us: per_device(): lag_table(vert_taps, (HEIGHT, EXT), a - HALO - i + MARGIN)]
    select_n x1 -> x0, other arithmetic: 2.67 us -> none  [per_device(): seams = jnp.where((w < PW) != (j < PW), bands, jnp.zeros((), jnp.bfloat16))]
    dot_general x2 -> x0, matrix products: 1.92 us -> none  [lag_table(): jnp.tensordot(filters, chosen, axes=1, preferred_element_type=jnp.float32)]
    convert_element_type x2 -> x0, other arithmetic: 1.43 us -> none  [the longest x1 0.73 us: per_device(): select = (lax.broadcasted_iota(jnp.int32, (slots, 1), 0) == slot.reshape(...]
    unnamed x11 -> x2, local copies, waits for them, and re-layouts: 2.47 us -> 3.24 us
where the time goes in v2:
time: 99.4 us; the launch traced here: 99.1 us
  Pallas kernels  95.3 us (96%)
  local copies, waits for them, and re-layouts  3.24 us (3%)
    pallas_call x1, Pallas kernels, per_device(): pl.pallas_call(kernel, out_shape=(jax.ShapeDtypeStruct(sky.shape, f32), j...  95.3 us
    unnamed x2, local copies, waits for them, and re-layouts  3.24 us

profile of v2, /device:TPU:1, one launch (start us, length us, event | category | flops | bytes accessed | tf_op | source)
XLA Modules:
  0.0 99.1 jit_solution(8177213936421394027)
XLA Ops:
  0.6 95.3 %shard_map.86 = (f32[64,128]{1,0:T(8,128)}, f32[2,128,512]{2,1,0:T(8,128)}) custom-call(s32[2,4,1,16]{3,2,1,0:T(1,128)} %bitcast.6, s32[2,4,16]{2,1,0:T(4,128)} %bitcast.7, f32[64,128]{1,0:T(8,128)} %bitcast.4, bf16[2,12,128,512]{3,2,1,0:T(8,128)(2,1)} %coeffs_far.1, f32[2,128,512]{2,1,0:T(8,128)} %observed_far.1, bf16[12,21]{1,0:T(8,128)(2,1)} %vert.1, ...), custom_call_target="tpu_custom_call" | custom-call | tf_op jit(solution)/shard_map/pallas_call | solution.py:554
  95.9 1.4 %copy.11 = f32[1,8,8,128]{3,2,1,0:T(8,128)} copy(f32[1,8,8,128]{3,2,1,0:T(8,128)} %bitcast.5) | data formatting | bytes 65536
  97.3 1.9 %copy.12 = f32[2,128,512]{2,1,0:T(8,128)} copy(f32[2,128,512]{2,1,0:T(8,128)} %get-tuple-element.9) | data formatting | bytes 1048576

commit v3 on v2

--- a/solution.py
+++ b/solution.py
@@ -25,9 +25,10 @@
 ROWS = HEIGHT // PH
 QCOLS = BREADTH // PW
 SIZE = PH * PW
-WIDE = SIZE + PW
 NEAR_ORDER = (0, 1, 7, 2, 6, 3, 5, 4)
 FAR_ORDER = (4, 3, 5, 2, 6, 1, 7)
+RELAYED = (0, 1, 7, 2, 6)
+PEERS = ((2, 0), (2, 1), (1, 0), (1, 1), (3, 0), (3, 1), (0, 1))
 VMEM_LIMIT = 60 * 1024 * 1024
 
 
@@ -100,20 +101,34 @@
         block = tile(lax.rem(x - dx + NX, NX) * NC + c_from, lax.rem(z - dz + NZ, NZ))
         return remote(block, block, cs.at[dz, dx], cr.at[dz, dx], at_exp(z, x, 1 - c))
 
+    def pass_on(dz, step):
+        block = tile(lax.rem(x - step + NX, NX) * NC + c, lax.rem(z - dz + NZ, NZ))
+        return remote(
+            block, block, xs.at[dz, 2], xr.at[dz, 2], at_exp(z, lax.rem(x + step, NX), c)
+        )
+
     for dz in FAR_ORDER:
         along_z(dz, False).start()
     early()
     for dz in NEAR_ORDER:
         if dz > 0:
             along_z(dz, True).wait_recv()
-        for dx in (2, 1, 3):
+        for dx in (1, 3) if dz in RELAYED else (2, 1, 3):
             along_x(dz, dx, False).start()
         to_twin(dz, 0, False).start()
     late()
-    for dz in NEAR_ORDER:
-        for dx in (1, 3, 2):
-            along_x(dz, dx, True).wait_recv()
-            to_twin(dz, dx, False).start()
+    for place_at in range(NZ + 2):
+        if place_at < NZ:
+            dz = NEAR_ORDER[place_at]
+            for dx in (1, 3):
+                along_x(dz, dx, True).wait_recv()
+                if dz in RELAYED and dx == (1 if dz % 2 == 0 else NX - 1):
+                    pass_on(dz, dx).start()
+                to_twin(dz, dx, False).start()
+        if place_at >= 2:
+            dz = NEAR_ORDER[place_at - 2]
+            along_x(dz, 2, True).wait_recv()
+            to_twin(dz, 2, False).start()
     for dz in NEAR_ORDER:
         for dx in range(NX):
             to_twin(dz, dx, True).wait_recv()
@@ -196,25 +211,94 @@
         down.wait_send()
 
 
-def reduce_patches(rows, select, extra, sky, sky_new, scratch):
+def across(outgoing, incoming, send_sem, recv_sem, dx, dc, back):
+    z, x, c, _ = place()
+    x_to, c_to = lax.rem(x + dx, NX), lax.rem(c + dc, NC)
+    x_from, c_from = (lax.rem(x - dx + NX, NX), c_to) if back else (x, c)
+    return remote(
+        outgoing.at[x_to * NC + c_to], incoming.at[x_from * NC + c_from],
+        send_sem.at[dx, dc], recv_sem.at[dx, dc], at_exp(z, x_to, c_to),
+    )
+
+
+def along_line(outgoing, incoming, send_sem, recv_sem, rel):
+    z, x, c, _ = place()
+    return remote(
+        outgoing.at[rel], incoming.at[rel], send_sem.at[rel], recv_sem.at[rel],
+        at_exp(lax.rem(z + rel, NZ), x, c),
+    )
+
+
+def send_marks(select, extra, marks_out, marks_in, send_sem, recv_sem):
+    z, x, c, _ = place()
+    col = x * NC + c
+    for half in range(2):
+        picked = jnp.dot(select[half], extra[...], preferred_element_type=jnp.float32)
+        marks_out[:, half * HALO:(half + 1) * HALO, :] = picked.astype(jnp.bfloat16).reshape(
+            COLS, HALO, PW
+        )
+    for dx, dc in PEERS:
+        across(marks_out, marks_in, send_sem, recv_sem, dx, dc, False).start()
+    marks_in[col] = marks_out[col]
+
+
+def take_marks(marks_out, marks_in, marks, count_out, count_in, sems):
+    send_sem, recv_sem, line_send, line_recv = sems
+    for dx, dc in PEERS:
+        across(marks_out, marks_in, send_sem, recv_sem, dx, dc, True).wait_recv()
+    for half in range(2):
+        arrived = marks_in[:, half * HALO:(half + 1) * HALO, :].reshape(COLS * HALO, PW)
+        turned = arrived.astype(jnp.float32).T[0:4 * PER_TILE].astype(jnp.bfloat16)
+        marks[half] = turned
+        many = jnp.dot(
+            turned, jnp.ones((COLS * HALO, PW), jnp.bfloat16), preferred_element_type=jnp.float32
+        )
+        for pos in range(4):
+            rel = (pos + 4 * (1 - half) + NZ - 2) % NZ
+            count_out[rel] = many[pos * PER_TILE:(pos + 1) * PER_TILE]
+    for rel in FAR_ORDER:
+        along_line(count_out, count_in, line_send, line_recv, rel).start()
+    for dx, dc in PEERS:
+        across(marks_out, marks_in, send_sem, recv_sem, dx, dc, False).wait_send()
+
+
+def take_counts(count_out, count_in, scale, sems):
+    _, _, line_send, line_recv = sems
+    total = count_out[0]
+    for rel in NEAR_ORDER[1:]:
+        along_line(count_out, count_in, line_send, line_recv, rel).wait_recv()
+        total = total + count_in[rel]
+    scale[...] = ETA / jnp.maximum(total, 1.0)
+    for rel in FAR_ORDER:
+        along_line(count_out, count_in, line_send, line_recv, rel).wait_send()
+
+
+def send_rims(rows, rim_out, rim_in, hs, hr):
+    _, _, _, y = place()
+    bands = lax.axis_size("sub")
+    rim_out[0] = rows[:, 0:HALO, :].astype(jnp.bfloat16)
+    rim_out[1] = rows[:, HALO + HEIGHT:EXT, :].astype(jnp.bfloat16)
+    up = remote(rim_out.at[0], rim_in.at[1], hs.at[0], hr.at[1], {"sub": y - 1})
+    down = remote(rim_out.at[1], rim_in.at[0], hs.at[1], hr.at[0], {"sub": y + 1})
+
+    @pl.when(y > 0)
+    def _():
+        up.start()
+
+    @pl.when(y < bands - 1)
+    def _():
+        down.start()
+
+    return up, down
+
+
+def reduce_patches(rows, rims, select, marks, get_scale, sky, sky_new, scratch):
     (rim_in, grad, stacked, outgoing, incoming, line_out, line_in), sems = scratch
-    hs, hr, axs, axr, bzs, bzr = sems
-    z, x, c, y = place()
+    axs, axr, bzs, bzr = sems
+    up, down = rims
+    _, x, c, y = place()
     bands = lax.axis_size("sub")
     col = x * NC + c
-    up = remote(rows.at[:, pl.ds(0, HALO), :], rim_in.at[1], hs.at[0], hr.at[1], {"sub": y - 1})
-    down = remote(
-        rows.at[:, pl.ds(HALO + HEIGHT, HALO), :], rim_in.at[0], hs.at[1], hr.at[0], {"sub": y + 1}
-    )
-
-    @pl.when(y > 0)
-    def _():
-        up.start()
-
-    @pl.when(y < bands - 1)
-    def _():
-        down.start()
-
     strips = [(p, q, (p * QCOLS + q) * HEIGHT) for p in range(PIECES) for q in range(QCOLS)]
     for p, q, at in strips:
         grad[at:at + HEIGHT, :] = rows[p, HALO:HALO + HEIGHT, q * PW:(q + 1) * PW]
@@ -223,74 +307,56 @@
     def _():
         down.wait_recv()
         for p, q, at in strips:
-            grad[at:at + HALO, :] += rim_in[0, p, :, q * PW:(q + 1) * PW]
+            grad[at:at + HALO, :] += rim_in[0, p, :, q * PW:(q + 1) * PW].astype(jnp.float32)
 
     @pl.when(y < bands - 1)
     def _():
         up.wait_recv()
         for p, q, at in strips:
-            grad[at + HEIGHT - HALO:at + HEIGHT, :] += rim_in[1, p, :, q * PW:(q + 1) * PW]
+            end = at + HEIGHT
+            grad[end - HALO:end, :] += rim_in[1, p, :, q * PW:(q + 1) * PW].astype(jnp.float32)
 
     for p, q, at in strips:
         for i in range(PH):
             lines = grad[pl.ds(at + i, ROWS, stride=PH), :]
             stacked[at // PH:at // PH + ROWS, i * PW:(i + 1) * PW] = lines.astype(jnp.bfloat16)
-    stacked[:, SIZE:] = extra[...]
-
-    def across(half, dx, dc, back):
-        x_to, c_to = lax.rem(x + dx, NX), lax.rem(c + dc, NC)
-        x_from, c_from = lax.rem(x - dx + NX, NX), lax.rem(c + dc, NC)
-        source = x_from * NC + c_from if back else col
-        return remote(
-            outgoing.at[half, x_to * NC + c_to], incoming.at[half, source],
-            axs.at[half, dx, dc], axr.at[half, dx, dc], at_exp(z, x_to, c_to),
+
+    def exchange(half, dx, dc, back):
+        return across(
+            outgoing.at[half], incoming.at[half], axs.at[half], axr.at[half], dx, dc, back
         )
 
-    peers = [(2, 0), (2, 1), (1, 0), (1, 1), (3, 0), (3, 1), (0, 1)]
     for half in range(2):
         picked = jnp.dot(
             select[half], stacked[...], preferred_element_type=jnp.float32
         ).astype(jnp.bfloat16)
-        outgoing[half] = picked.reshape(COLS, HALO, WIDE)
-        for dx, dc in peers:
-            across(half, dx, dc, False).start()
+        outgoing[half] = picked.reshape(COLS, HALO, SIZE)
+        for dx, dc in PEERS:
+            exchange(half, dx, dc, False).start()
         incoming[half, col] = outgoing[half, col]
-
-    def along_z(rel, start_at):
-        return remote(
-            line_out.at[rel], line_in.at[rel], bzs.at[rel], bzr.at[rel],
-            at_exp(lax.rem(z + rel, NZ), x, c),
-        )
-
     for half in range(2):
-        for dx, dc in peers[::-1]:
-            across(half, dx, dc, True).wait_recv()
-        arrived = incoming[half].reshape(COLS * HALO, WIDE)
-        marks = arrived[:, SIZE:].astype(jnp.float32).T[0:4 * PER_TILE].astype(jnp.bfloat16)
-        totals = jnp.dot(marks, arrived[:, :SIZE], preferred_element_type=jnp.float32)
-        many = jnp.dot(
-            marks, jnp.ones((COLS * HALO, PW), jnp.bfloat16), preferred_element_type=jnp.float32
-        )
+        for dx, dc in PEERS[::-1]:
+            exchange(half, dx, dc, True).wait_recv()
+        arrived = incoming[half].reshape(COLS * HALO, SIZE)
+        totals = jnp.dot(marks[half], arrived, preferred_element_type=jnp.float32)
         for pos in (2, 1, 3, 0) if half == 0 else (0, 3, 1, 2):
             rel = (pos + 4 * (1 - half) + NZ - 2) % NZ
-            line = slice(pos * PER_TILE, (pos + 1) * PER_TILE)
-            line_out[rel, :, 0:SIZE] = totals[line].astype(jnp.bfloat16)
-            line_out[rel, :, SIZE:] = many[line].astype(jnp.bfloat16)
+            line_out[rel] = totals[pos * PER_TILE:(pos + 1) * PER_TILE].astype(jnp.bfloat16)
             if rel > 0:
-                along_z(rel, True).start()
+                along_line(line_out, line_in, bzs, bzr, rel).start()
+    scale = get_scale()
     total = line_out[0].astype(jnp.float32)
     for rel in NEAR_ORDER[1:]:
-        along_z(rel, False).wait_recv()
+        along_line(line_out, line_in, bzs, bzr, rel).wait_recv()
         total = total + line_in[rel].astype(jnp.float32)
-    scale = ETA / jnp.maximum(total[:, SIZE:], 1.0)
     for i in range(PH):
         old = sky[pl.ds(i, PER_TILE, stride=PH), :]
         sky_new[pl.ds(i, PER_TILE, stride=PH), :] = old - scale * total[:, i * PW:(i + 1) * PW]
     for half in range(2):
-        for dx, dc in peers:
-            across(half, dx, dc, False).wait_send()
+        for dx, dc in PEERS:
+            exchange(half, dx, dc, False).wait_send()
     for rel in range(1, NZ):
-        along_z(rel, False).wait_send()
+        along_line(line_out, line_in, bzs, bzr, rel).wait_send()
 
     @pl.when(y > 0)
     def _():
@@ -430,7 +496,7 @@
                 )
         return carry
 
-    lax.fori_loop(0, MODES, forward, 0)
+    lax.fori_loop(0, MODES, forward, 0, unroll=MODES)
     clipped[...] = jnp.clip(model[...], -DELTA, DELTA)
 
     def adjoint(m, carry):
@@ -451,7 +517,7 @@
                 )
         return carry
 
-    lax.fori_loop(0, MODES, adjoint, 0)
+    lax.fori_loop(0, MODES, adjoint, 0, unroll=MODES)
     turned = jnp.concatenate([wide[m] for m in range(MODES)], axis=1)
     for p in range(PIECES):
         rows[p] = jnp.dot(turned, back[p], preferred_element_type=jnp.float32)
@@ -460,9 +526,11 @@
 def kernel(owners, offsets, sky, coeffs_far, observed_far, vert, horiz, sky_out, clipped, *scratch):
     (
         coeffs, observed, base, tall, wide, bands, seams, own_rows, off_rows, select, extra,
-        table, rim_out, rim_in, ext, smooth, back, model, rows, sky_mid, *scratch
+        table, rim_out, rim_in, ext, smooth, back, model, rows, sky_mid,
+        marks_out, marks_in, marks, count_out, count_in, scale, adj_out, *scratch
     ) = scratch
-    load, fetch_sems, reduce_refs, reduce_sems = scratch[0], scratch[1:9], scratch[9:16], scratch[16:]
+    load, mark_sems, fetch_sems = scratch[0], scratch[1:5], scratch[5:13]
+    adj_in, reduce_refs, reduce_sems = scratch[13], scratch[13:20], scratch[20:]
     loads = [
         pltpu.make_async_copy(coeffs_far, coeffs, load.at[0]),
         pltpu.make_async_copy(observed_far, observed, load.at[1]),
@@ -490,14 +558,37 @@
         spread_tiles(table, sems[:6], early if first else nothing, late if first else nothing)
         fetch_image(owners, offsets, table, ext, rim_out, rim_in, *sems[6:])
         if first:
+            send_marks(select, extra, marks_out, marks_in, *mark_sems[:2])
             for copy in loads:
                 copy.wait()
         compute(ext, coeffs, observed, (tall, wide, bands, seams), clipped, rows, (smooth, back, model))
         sems = [ref.at[step] for ref in reduce_sems]
+        rims = send_rims(rows, adj_out, adj_in, *sems[:2])
+        if first:
+            take_marks(marks_out, marks_in, marks, count_out, count_in, mark_sems)
+
+        def get_scale():
+            if first:
+                take_counts(count_out, count_in, scale, mark_sems)
+            return scale[...]
+
         before, after = (sky, sky_mid) if first else (sky_mid, sky_out)
-        reduce_patches(rows, select, extra, before, after, (reduce_refs, sems))
+        reduce_patches(rows, rims, select, marks, get_scale, before, after, (reduce_refs, sems[2:]))
         if first:
             own_tile(sky_mid, table)
+
+
+def copy_out(sky_far, clipped_far, sky_out, clipped_out, sky, clipped, load, store):
+    pairs = ((clipped_far, clipped, clipped_out), (sky_far, sky, sky_out))
+    inward = [pltpu.make_async_copy(a, b, load.at[i]) for i, (a, b, _) in enumerate(pairs)]
+    outward = [pltpu.make_async_copy(b, c, store.at[i]) for i, (_, b, c) in enumerate(pairs)]
+    for copy in inward:
+        copy.start()
+    for came, goes in zip(inward, outward):
+        came.wait()
+        goes.start()
+    for copy in outward:
+        copy.wait()
 
 
 def per_device(sky_map, coeffs, observed, vert_taps, horiz_taps, owner_ids, offset):
@@ -527,7 +618,18 @@
         pltpu.VMEM((PIECES, HEIGHT, BREADTH), f32),
         pltpu.VMEM((PIECES, EXT, BREADTH), f32),
         pltpu.VMEM((PER_TILE * PH, PW), f32),
+        pltpu.VMEM((COLS, 2 * HALO, PW), bf16),
+        pltpu.VMEM((COLS, 2 * HALO, PW), bf16),
+        pltpu.VMEM((2, 4 * PER_TILE, COLS * HALO), bf16),
+        pltpu.VMEM((NZ, PER_TILE, PW), f32),
+        pltpu.VMEM((NZ, PER_TILE, PW), f32),
+        pltpu.VMEM((PER_TILE, PW), f32),
+        pltpu.VMEM((2, PIECES, HALO, BREADTH), bf16),
         dma((2,)),
+        dma((NX, NC)),
+        dma((NX, NC)),
+        dma((NZ,)),
+        dma((NZ,)),
         dma((STEPS, NZ)),
         dma((STEPS, NZ)),
         dma((STEPS, NZ, NX)),
@@ -536,13 +638,13 @@
         dma((STEPS, NZ, NX)),
         dma((STEPS, 2)),
         dma((STEPS, 2)),
-        pltpu.VMEM((2, PIECES, HALO, BREADTH), f32),
+        pltpu.VMEM((2, PIECES, HALO, BREADTH), bf16),
         pltpu.VMEM((PIECES * QCOLS * HEIGHT, PW), f32),
-        pltpu.VMEM((count, WIDE), bf16),
-        pltpu.VMEM((2, COLS, HALO, WIDE), bf16),
-        pltpu.VMEM((2, COLS, HALO, WIDE), bf16),
-        pltpu.VMEM((NZ, PER_TILE, WIDE), bf16),
-        pltpu.VMEM((NZ, PER_TILE, WIDE), bf16),
+        pltpu.VMEM((count, SIZE), bf16),
+        pltpu.VMEM((2, COLS, HALO, SIZE), bf16),
+        pltpu.VMEM((2, COLS, HALO, SIZE), bf16),
+        pltpu.VMEM((NZ, PER_TILE, SIZE), bf16),
+        pltpu.VMEM((NZ, PER_TILE, SIZE), bf16),
         dma((STEPS, 2)),
         dma((STEPS, 2)),
         dma((STEPS, 2, NX, NC)),
@@ -564,6 +666,17 @@
             vmem_limit_bytes=VMEM_LIMIT, collective_id=0, has_side_effects=True
         ),
     )(owner_ids.transpose(0, 2, 3, 1), offset.transpose(0, 2, 1), sky, coeffs, observed, vert_taps, horiz_taps)
+    sky_new, clipped = pl.pallas_call(
+        copy_out,
+        out_shape=(
+            jax.ShapeDtypeStruct(sky.shape, f32),
+            jax.ShapeDtypeStruct(observed.shape, f32),
+        ),
+        in_specs=[pl.BlockSpec(memory_space=far)] * 2,
+        out_specs=(pl.BlockSpec(memory_space=far), pl.BlockSpec(memory_space=far)),
+        scratch_shapes=[pltpu.VMEM(sky.shape, f32), pltpu.VMEM(observed.shape, f32), dma((2,)), dma((2,))],
+        compiler_params=pltpu.CompilerParams(vmem_limit_bytes=VMEM_LIMIT),
+    )(sky_new, clipped)
     return sky_new.reshape(sky_map.shape), clipped
 
 

time: 99.4 us -> 91.2 us (0.918)
  Pallas kernels: 95.3 us -> 90.4 us
  local copies, waits for them, and re-layouts: 3.24 us -> 0 us
    pallas_call x1, Pallas kernels: 95.3 us -> 88.5 us  [per_device(): pl.pallas_call(kernel, out_shape=(jax.ShapeDtypeStruct(sky.shape, f32), j...]
    unnamed x2 -> x0, local copies, waits for them, and re-layouts: 3.24 us -> none
    pallas_call x0 -> x1, Pallas kernels: none -> 1.87 us  [per_device(): pl.pallas_call(copy_out, out_shape=(jax.ShapeDtypeStruct(sky.shape, f32),...]
where the time goes in v3:
time: 91.2 us; the launch traced here: 91 us
  Pallas kernels  90.4 us (99%)
    pallas_call x1, Pallas kernels, per_device(): pl.pallas_call(kernel, out_shape=(jax.ShapeDtypeStruct(sky.shape, f32), j...  88.5 us
    pallas_call x1, Pallas kernels, per_device(): pl.pallas_call(copy_out, out_shape=(jax.ShapeDtypeStruct(sky.shape, f32),...  1.87 us

profile of v3, /device:TPU:1, one launch (start us, length us, event | category | flops | bytes accessed | tf_op | source)
XLA Modules:
  0.0 91.0 jit_solution(16450061006402018564)
XLA Ops:
  0.6 88.5 %shard_map.86 = (f32[64,128]{1,0:T(8,128)}, f32[2,128,512]{2,1,0:T(8,128)}) custom-call(s32[2,4,1,16]{3,2,1,0:T(1,128)} %bitcast.5, s32[2,4,16]{2,1,0:T(4,128)} %bitcast.6, f32[64,128]{1,0:T(8,128)} %bitcast.4, bf16[2,12,128,512]{3,2,1,0:T(8,128)(2,1)} %coeffs_far.1, f32[2,128,512]{2,1,0:T(8,128)} %observed_far.1, bf16[12,21]{1,0:T(8,128)(2,1)} %vert.1, ...), custom_call_target="tpu_custom_call" | custom-call | tf_op jit(solution)/shard_map/pallas_call | solution.py:656
  89.2 1.9 %shard_map.87 = (f32[64,128]{1,0:T(8,128)}, f32[2,128,512]{2,1,0:T(8,128)}) custom-call(f32[64,128]{1,0:T(8,128)} %get-tuple-element.6.sky_far, f32[2,128,512]{2,1,0:T(8,128)} %get-tuple-element.7.clipped_far), custom_call_target="tpu_custom_call" | custom-call | tf_op jit(solution)/shard_map/pallas_call | solution.py:669

commit v4 on v3

--- a/solution.py
+++ b/solution.py
@@ -27,7 +27,9 @@
 SIZE = PH * PW
 NEAR_ORDER = (0, 1, 7, 2, 6, 3, 5, 4)
 FAR_ORDER = (4, 3, 5, 2, 6, 1, 7)
-RELAYED = (0, 1, 7, 2, 6)
+CHUNKS = ((4, 3), (5, 2), (6, 1), (7, 0))
+N_CHUNKS = len(CHUNKS)
+CHUNK_ROWS = 4 * len(CHUNKS[0])
 PEERS = ((2, 0), (2, 1), (1, 0), (1, 1), (3, 0), (3, 1), (0, 1))
 VMEM_LIMIT = 60 * 1024 * 1024
 
@@ -101,34 +103,20 @@
         block = tile(lax.rem(x - dx + NX, NX) * NC + c_from, lax.rem(z - dz + NZ, NZ))
         return remote(block, block, cs.at[dz, dx], cr.at[dz, dx], at_exp(z, x, 1 - c))
 
-    def pass_on(dz, step):
-        block = tile(lax.rem(x - step + NX, NX) * NC + c, lax.rem(z - dz + NZ, NZ))
-        return remote(
-            block, block, xs.at[dz, 2], xr.at[dz, 2], at_exp(z, lax.rem(x + step, NX), c)
-        )
-
     for dz in FAR_ORDER:
         along_z(dz, False).start()
     early()
     for dz in NEAR_ORDER:
         if dz > 0:
             along_z(dz, True).wait_recv()
-        for dx in (1, 3) if dz in RELAYED else (2, 1, 3):
+        for dx in (2, 1, 3):
             along_x(dz, dx, False).start()
         to_twin(dz, 0, False).start()
     late()
-    for place_at in range(NZ + 2):
-        if place_at < NZ:
-            dz = NEAR_ORDER[place_at]
-            for dx in (1, 3):
-                along_x(dz, dx, True).wait_recv()
-                if dz in RELAYED and dx == (1 if dz % 2 == 0 else NX - 1):
-                    pass_on(dz, dx).start()
-                to_twin(dz, dx, False).start()
-        if place_at >= 2:
-            dz = NEAR_ORDER[place_at - 2]
-            along_x(dz, 2, True).wait_recv()
-            to_twin(dz, 2, False).start()
+    for dz in NEAR_ORDER:
+        for dx in (1, 3, 2):
+            along_x(dz, dx, True).wait_recv()
+            to_twin(dz, dx, False).start()
     for dz in NEAR_ORDER:
         for dx in range(NX):
             to_twin(dz, dx, True).wait_recv()
@@ -211,12 +199,14 @@
         down.wait_send()
 
 
-def across(outgoing, incoming, send_sem, recv_sem, dx, dc, back):
+def across(outgoing, incoming, send_sem, recv_sem, dx, dc, back, every=False):
     z, x, c, _ = place()
     x_to, c_to = lax.rem(x + dx, NX), lax.rem(c + dc, NC)
     x_from, c_from = (lax.rem(x - dx + NX, NX), c_to) if back else (x, c)
+    to_at, from_at = x_to * NC + c_to, x_from * NC + c_from
     return remote(
-        outgoing.at[x_to * NC + c_to], incoming.at[x_from * NC + c_from],
+        outgoing.at[:, to_at] if every else outgoing.at[to_at],
+        incoming.at[:, from_at] if every else incoming.at[from_at],
         send_sem.at[dx, dc], recv_sem.at[dx, dc], at_exp(z, x_to, c_to),
     )
 
@@ -232,34 +222,31 @@
 def send_marks(select, extra, marks_out, marks_in, send_sem, recv_sem):
     z, x, c, _ = place()
     col = x * NC + c
-    for half in range(2):
-        picked = jnp.dot(select[half], extra[...], preferred_element_type=jnp.float32)
-        marks_out[:, half * HALO:(half + 1) * HALO, :] = picked.astype(jnp.bfloat16).reshape(
-            COLS, HALO, PW
-        )
+    for chunk in range(N_CHUNKS):
+        picked = jnp.dot(select[chunk], extra[...], preferred_element_type=jnp.float32)
+        marks_out[chunk] = picked.reshape(COLS, CHUNK_ROWS, PW).astype(jnp.bfloat16)
     for dx, dc in PEERS:
-        across(marks_out, marks_in, send_sem, recv_sem, dx, dc, False).start()
-    marks_in[col] = marks_out[col]
+        across(marks_out, marks_in, send_sem, recv_sem, dx, dc, False, True).start()
+    marks_in[:, col] = marks_out[:, col]
 
 
 def take_marks(marks_out, marks_in, marks, count_out, count_in, sems):
     send_sem, recv_sem, line_send, line_recv = sems
     for dx, dc in PEERS:
-        across(marks_out, marks_in, send_sem, recv_sem, dx, dc, True).wait_recv()
-    for half in range(2):
-        arrived = marks_in[:, half * HALO:(half + 1) * HALO, :].reshape(COLS * HALO, PW)
-        turned = arrived.astype(jnp.float32).T[0:4 * PER_TILE].astype(jnp.bfloat16)
-        marks[half] = turned
+        across(marks_out, marks_in, send_sem, recv_sem, dx, dc, True, True).wait_recv()
+    for chunk in range(N_CHUNKS):
+        arrived = marks_in[chunk].astype(jnp.float32).reshape(COLS * CHUNK_ROWS, PW)
+        turned = arrived.T[0:2 * PER_TILE].astype(jnp.bfloat16)
+        marks[chunk] = turned
         many = jnp.dot(
-            turned, jnp.ones((COLS * HALO, PW), jnp.bfloat16), preferred_element_type=jnp.float32
+            turned, jnp.ones((COLS * CHUNK_ROWS, PW), jnp.bfloat16), preferred_element_type=jnp.float32
         )
-        for pos in range(4):
-            rel = (pos + 4 * (1 - half) + NZ - 2) % NZ
+        for pos, rel in enumerate(CHUNKS[chunk]):
             count_out[rel] = many[pos * PER_TILE:(pos + 1) * PER_TILE]
     for rel in FAR_ORDER:
         along_line(count_out, count_in, line_send, line_recv, rel).start()
     for dx, dc in PEERS:
-        across(marks_out, marks_in, send_sem, recv_sem, dx, dc, False).wait_send()
+        across(marks_out, marks_in, send_sem, recv_sem, dx, dc, False, True).wait_send()
 
 
 def take_counts(count_out, count_in, scale, sems):
@@ -293,54 +280,50 @@
 
 
 def reduce_patches(rows, rims, select, marks, get_scale, sky, sky_new, scratch):
-    (rim_in, grad, stacked, outgoing, incoming, line_out, line_in), sems = scratch
+    (rim_in, stacked, outgoing, incoming, line_out, line_in), sems = scratch
     axs, axr, bzs, bzr = sems
     up, down = rims
     _, x, c, y = place()
     bands = lax.axis_size("sub")
     col = x * NC + c
-    strips = [(p, q, (p * QCOLS + q) * HEIGHT) for p in range(PIECES) for q in range(QCOLS)]
-    for p, q, at in strips:
-        grad[at:at + HEIGHT, :] = rows[p, HALO:HALO + HEIGHT, q * PW:(q + 1) * PW]
+    strips = range(PIECES * QCOLS)
 
     @pl.when(y > 0)
     def _():
         down.wait_recv()
-        for p, q, at in strips:
-            grad[at:at + HALO, :] += rim_in[0, p, :, q * PW:(q + 1) * PW].astype(jnp.float32)
+        for n in strips:
+            rows[n, HALO:2 * HALO, :] += rim_in[0, n].astype(jnp.float32)
 
     @pl.when(y < bands - 1)
     def _():
         up.wait_recv()
-        for p, q, at in strips:
-            end = at + HEIGHT
-            grad[end - HALO:end, :] += rim_in[1, p, :, q * PW:(q + 1) * PW].astype(jnp.float32)
-
-    for p, q, at in strips:
+        for n in strips:
+            rows[n, HEIGHT:HALO + HEIGHT, :] += rim_in[1, n].astype(jnp.float32)
+
+    for n in strips:
         for i in range(PH):
-            lines = grad[pl.ds(at + i, ROWS, stride=PH), :]
-            stacked[at // PH:at // PH + ROWS, i * PW:(i + 1) * PW] = lines.astype(jnp.bfloat16)
-
-    def exchange(half, dx, dc, back):
+            lines = rows[n, pl.ds(HALO + i, ROWS, stride=PH), :]
+            stacked[n * ROWS:(n + 1) * ROWS, i * PW:(i + 1) * PW] = lines.astype(jnp.bfloat16)
+
+    def exchange(chunk, dx, dc, back):
         return across(
-            outgoing.at[half], incoming.at[half], axs.at[half], axr.at[half], dx, dc, back
+            outgoing.at[chunk], incoming.at[chunk], axs.at[chunk], axr.at[chunk], dx, dc, back
         )
 
-    for half in range(2):
-        picked = jnp.dot(
-            select[half], stacked[...], preferred_element_type=jnp.float32
-        ).astype(jnp.bfloat16)
-        outgoing[half] = picked.reshape(COLS, HALO, SIZE)
+    for chunk in range(N_CHUNKS):
+        picked = jnp.dot(select[chunk], stacked[...], preferred_element_type=jnp.float32)
+        outgoing[chunk] = picked.reshape(COLS, CHUNK_ROWS, SIZE).astype(jnp.bfloat16)
         for dx, dc in PEERS:
-            exchange(half, dx, dc, False).start()
-        incoming[half, col] = outgoing[half, col]
-    for half in range(2):
+            exchange(chunk, dx, dc, False).start()
+        incoming[chunk, col] = outgoing[chunk, col]
+    for chunk in range(N_CHUNKS):
         for dx, dc in PEERS[::-1]:
-            exchange(half, dx, dc, True).wait_recv()
-        arrived = incoming[half].reshape(COLS * HALO, SIZE)
-        totals = jnp.dot(marks[half], arrived, preferred_element_type=jnp.float32)
-        for pos in (2, 1, 3, 0) if half == 0 else (0, 3, 1, 2):
-            rel = (pos + 4 * (1 - half) + NZ - 2) % NZ
+            exchange(chunk, dx, dc, True).wait_recv()
+        arrived = incoming[chunk].astype(jnp.float32).reshape(COLS * CHUNK_ROWS, SIZE)
+        totals = jnp.dot(
+            marks[chunk], arrived.astype(jnp.bfloat16), preferred_element_type=jnp.float32
+        )
+        for pos, rel in enumerate(CHUNKS[chunk]):
             line_out[rel] = totals[pos * PER_TILE:(pos + 1) * PER_TILE].astype(jnp.bfloat16)
             if rel > 0:
                 along_line(line_out, line_in, bzs, bzr, rel).start()
@@ -352,9 +335,9 @@
     for i in range(PH):
         old = sky[pl.ds(i, PER_TILE, stride=PH), :]
         sky_new[pl.ds(i, PER_TILE, stride=PH), :] = old - scale * total[:, i * PW:(i + 1) * PW]
-    for half in range(2):
+    for chunk in range(N_CHUNKS):
         for dx, dc in PEERS:
-            exchange(half, dx, dc, False).wait_send()
+            exchange(chunk, dx, dc, False).wait_send()
     for rel in range(1, NZ):
         along_line(line_out, line_in, bzs, bzr, rel).wait_send()
 
@@ -464,15 +447,17 @@
     across = own_along[0:1, :]
 
     def turned(owner):
-        return lax.rem(owner // COLS - z + NZ + 2, NZ)
+        far = lax.rem(owner // COLS - z + NZ + NZ // 2, NZ)
+        return jnp.where(far < NZ // 2, 2 * far, 2 * (NZ - far) - 1)
 
     spin = turned(across)
-    half, pos = 1 - spin // 4, lax.rem(spin, 4)
+    chunk, pos = spin // 2, lax.rem(spin, 2)
     piece = along[0:1, :] // per_piece
-    slot = ((half * COLS + lax.rem(across, COLS)) * 4 + pos) * 4 + piece * 2 + rank
-    for h in range(2):
-        select[h] = (down + h * count == slot).astype(jnp.bfloat16)
-    mark = lax.rem(turned(own), 4) * PER_TILE + off_rows[...]
+    slot = ((chunk * COLS + lax.rem(across, COLS)) * 2 + pos) * 4 + piece * 2 + rank
+    size = COLS * CHUNK_ROWS
+    for h in range(N_CHUNKS):
+        select[h] = (down[0:size] + h * size == slot).astype(jnp.bfloat16)
+    mark = lax.rem(turned(own), 2) * PER_TILE + off_rows[...]
     extra[...] = (mark == along).astype(jnp.bfloat16)
 
 
@@ -520,7 +505,9 @@
     lax.fori_loop(0, MODES, adjoint, 0, unroll=MODES)
     turned = jnp.concatenate([wide[m] for m in range(MODES)], axis=1)
     for p in range(PIECES):
-        rows[p] = jnp.dot(turned, back[p], preferred_element_type=jnp.float32)
+        total = jnp.dot(turned, back[p], preferred_element_type=jnp.float32)
+        for q in range(QCOLS):
+            rows[p * QCOLS + q] = total[:, q * PW:(q + 1) * PW]
 
 
 def kernel(owners, offsets, sky, coeffs_far, observed_far, vert, horiz, sky_out, clipped, *scratch):
@@ -530,7 +517,7 @@
         marks_out, marks_in, marks, count_out, count_in, scale, adj_out, *scratch
     ) = scratch
     load, mark_sems, fetch_sems = scratch[0], scratch[1:5], scratch[5:13]
-    adj_in, reduce_refs, reduce_sems = scratch[13], scratch[13:20], scratch[20:]
+    adj_in, reduce_refs, reduce_sems = scratch[13], scratch[13:19], scratch[19:]
     loads = [
         pltpu.make_async_copy(coeffs_far, coeffs, load.at[0]),
         pltpu.make_async_copy(observed_far, observed, load.at[1]),
@@ -607,7 +594,7 @@
         pltpu.VMEM((MODES, side, side), bf16),
         pltpu.VMEM((count, PW), i32),
         pltpu.VMEM((count, PW), i32),
-        pltpu.VMEM((2, count, count), bf16),
+        pltpu.VMEM((N_CHUNKS, COLS * CHUNK_ROWS, count), bf16),
         pltpu.VMEM((count, PW), bf16),
         pltpu.VMEM((COLS * NZ * PER_TILE, PH, PW), bf16),
         pltpu.VMEM((2, PIECES, HALO, BREADTH), bf16),
@@ -616,15 +603,15 @@
         pltpu.VMEM((MODES, PIECES * HEIGHT, BREADTH), bf16),
         pltpu.VMEM((PIECES, MODES * HEIGHT, BREADTH), bf16),
         pltpu.VMEM((PIECES, HEIGHT, BREADTH), f32),
-        pltpu.VMEM((PIECES, EXT, BREADTH), f32),
+        pltpu.VMEM((PIECES * QCOLS, EXT, PW), f32),
         pltpu.VMEM((PER_TILE * PH, PW), f32),
-        pltpu.VMEM((COLS, 2 * HALO, PW), bf16),
-        pltpu.VMEM((COLS, 2 * HALO, PW), bf16),
-        pltpu.VMEM((2, 4 * PER_TILE, COLS * HALO), bf16),
+        pltpu.VMEM((N_CHUNKS, COLS, CHUNK_ROWS, PW), bf16),
+        pltpu.VMEM((N_CHUNKS, COLS, CHUNK_ROWS, PW), bf16),
+        pltpu.VMEM((N_CHUNKS, 2 * PER_TILE, COLS * CHUNK_ROWS), bf16),
         pltpu.VMEM((NZ, PER_TILE, PW), f32),
         pltpu.VMEM((NZ, PER_TILE, PW), f32),
         pltpu.VMEM((PER_TILE, PW), f32),
-        pltpu.VMEM((2, PIECES, HALO, BREADTH), bf16),
+        pltpu.VMEM((2, PIECES * QCOLS, HALO, PW), bf16),
         dma((2,)),
         dma((NX, NC)),
         dma((NX, NC)),
@@ -638,17 +625,16 @@
         dma((STEPS, NZ, NX)),
         dma((STEPS, 2)),
         dma((STEPS, 2)),
-        pltpu.VMEM((2, PIECES, HALO, BREADTH), bf16),
-        pltpu.VMEM((PIECES * QCOLS * HEIGHT, PW), f32),
+        pltpu.VMEM((2, PIECES * QCOLS, HALO, PW), bf16),
         pltpu.VMEM((count, SIZE), bf16),
-        pltpu.VMEM((2, COLS, HALO, SIZE), bf16),
-        pltpu.VMEM((2, COLS, HALO, SIZE), bf16),
+        pltpu.VMEM((N_CHUNKS, COLS, CHUNK_ROWS, SIZE), bf16),
+        pltpu.VMEM((N_CHUNKS, COLS, CHUNK_ROWS, SIZE), bf16),
         pltpu.VMEM((NZ, PER_TILE, SIZE), bf16),
         pltpu.VMEM((NZ, PER_TILE, SIZE), bf16),
         dma((STEPS, 2)),
         dma((STEPS, 2)),
-        dma((STEPS, 2, NX, NC)),
-        dma((STEPS, 2, NX, NC)),
+        dma((STEPS, N_CHUNKS, NX, NC)),
+        dma((STEPS, N_CHUNKS, NX, NC)),
         dma((STEPS, NZ)),
         dma((STEPS, NZ)),
     ]

time: 91.2 us -> 85 us (0.932)
  Pallas kernels: 90.4 us -> 84.2 us
    pallas_call x1, Pallas kernels: 88.5 us -> 82.3 us  [per_device(): pl.pallas_call(kernel, out_shape=(jax.ShapeDtypeStruct(sky.shape, f32), j...]
where the time goes in v4:
time: 85 us; the launch traced here: 84.9 us
  Pallas kernels  84.2 us (99%)
    pallas_call x1, Pallas kernels, per_device(): pl.pallas_call(kernel, out_shape=(jax.ShapeDtypeStruct(sky.shape, f32), j...  82.3 us
    pallas_call x1, Pallas kernels, per_device(): pl.pallas_call(copy_out, out_shape=(jax.ShapeDtypeStruct(sky.shape, f32),...  1.87 us

profile of v4, /device:TPU:1, one launch (start us, length us, event | category | flops | bytes accessed | tf_op | source)
XLA Modules:
  0.0 84.9 jit_solution(11738214000829477309)
XLA Ops:
  0.6 82.3 %shard_map.86 = (f32[64,128]{1,0:T(8,128)}, f32[2,128,512]{2,1,0:T(8,128)}) custom-call(s32[2,4,1,16]{3,2,1,0:T(1,128)} %bitcast.5, s32[2,4,16]{2,1,0:T(4,128)} %bitcast.6, f32[64,128]{1,0:T(8,128)} %bitcast.4, bf16[2,12,128,512]{3,2,1,0:T(8,128)(2,1)} %coeffs_far.1, f32[2,128,512]{2,1,0:T(8,128)} %observed_far.1, bf16[12,21]{1,0:T(8,128)(2,1)} %vert.1, ...), custom_call_target="tpu_custom_call" | custom-call | tf_op jit(solution)/shard_map/pallas_call | solution.py:642
  83.0 1.9 %shard_map.87 = (f32[64,128]{1,0:T(8,128)}, f32[2,128,512]{2,1,0:T(8,128)}) custom-call(f32[64,128]{1,0:T(8,128)} %get-tuple-element.6.sky_far, f32[2,128,512]{2,1,0:T(8,128)} %get-tuple-element.7.clipped_far), custom_call_target="tpu_custom_call" | custom-call | tf_op jit(solution)/shard_map/pallas_call | solution.py:655

commit v5 on v4

--- a/solution.py
+++ b/solution.py
@@ -18,7 +18,9 @@
 HEIGHT = 128
 BREADTH = 512
 HALO = 16
-EXT = HEIGHT + 2 * HALO
+TALL = HEIGHT + 2 * HALO
+REACH = 2 * HALO
+EXT = HEIGHT + 2 * REACH
 PER_TILE = 8
 PH = 8
 PW = 128
@@ -140,9 +142,9 @@
                 both.append(table[tile * PER_TILE + offsets[p, q, r]].astype(jnp.float32))
             block = jnp.concatenate(both, axis=0).astype(jnp.bfloat16)
             if isinstance(pair, int):
-                start = HALO + pair * 2 * PH
+                start = REACH + pair * 2 * PH
             else:
-                start = pl.multiple_of(HALO + pair * 2 * PH, 2 * PH)
+                start = pl.multiple_of(REACH + pair * 2 * PH, 2 * PH)
             ext[p, pl.ds(start, 2 * PH), q * PW:(q + 1) * PW] = block
 
 
@@ -150,10 +152,10 @@
     _, _, _, y = place()
     bands = lax.axis_size("sub")
     pairs = ROWS // 2
-    gather_rows(owners, offsets, table, ext, 0)
-    gather_rows(owners, offsets, table, ext, pairs - 1)
-    rim_out[0] = ext[:, HALO:2 * HALO, :]
-    rim_out[1] = ext[:, HEIGHT:HEIGHT + HALO, :]
+    for pair in (0, 1, pairs - 2, pairs - 1):
+        gather_rows(owners, offsets, table, ext, pair)
+    rim_out[0] = ext[:, REACH:2 * REACH, :]
+    rim_out[1] = ext[:, HEIGHT:HEIGHT + REACH, :]
     up = remote(rim_out.at[0], rim_in.at[1], hs.at[0], hr.at[1], {"sub": y - 1})
     down = remote(rim_out.at[1], rim_in.at[0], hs.at[1], hr.at[0], {"sub": y + 1})
 
@@ -169,26 +171,26 @@
         gather_rows(owners, offsets, table, ext, pair)
         return carry
 
-    lax.fori_loop(1, pairs - 1, more, 0)
-    none = jnp.zeros((PIECES, HALO, BREADTH), jnp.bfloat16)
+    lax.fori_loop(2, pairs - 2, more, 0)
+    none = jnp.zeros((PIECES, REACH, BREADTH), jnp.bfloat16)
 
     @pl.when(y > 0)
     def _():
         down.wait_recv()
-        ext[:, 0:HALO, :] = rim_in[0]
+        ext[:, 0:REACH, :] = rim_in[0]
 
     @pl.when(y == 0)
     def _():
-        ext[:, 0:HALO, :] = none
+        ext[:, 0:REACH, :] = none
 
     @pl.when(y < bands - 1)
     def _():
         up.wait_recv()
-        ext[:, HALO + HEIGHT:EXT, :] = rim_in[1]
+        ext[:, REACH + HEIGHT:EXT, :] = rim_in[1]
 
     @pl.when(y == bands - 1)
     def _():
-        ext[:, HALO + HEIGHT:EXT, :] = none
+        ext[:, REACH + HEIGHT:EXT, :] = none
 
     @pl.when(y > 0)
     def _():
@@ -260,49 +262,74 @@
         along_line(count_out, count_in, line_send, line_recv, rel).wait_send()
 
 
-def send_rims(rows, rim_out, rim_in, hs, hr):
+def share_rows(coeffs_far, observed_far, coeffs, observed, hs, hr):
     _, _, _, y = place()
     bands = lax.axis_size("sub")
-    rim_out[0] = rows[:, 0:HALO, :].astype(jnp.bfloat16)
-    rim_out[1] = rows[:, HALO + HEIGHT:EXT, :].astype(jnp.bfloat16)
-    up = remote(rim_out.at[0], rim_in.at[1], hs.at[0], hr.at[1], {"sub": y - 1})
-    down = remote(rim_out.at[1], rim_in.at[0], hs.at[1], hr.at[0], {"sub": y + 1})
-
-    @pl.when(y > 0)
-    def _():
-        up.start()
-
-    @pl.when(y < bands - 1)
-    def _():
-        down.start()
-
-    return up, down
-
-
-def reduce_patches(rows, rims, select, marks, get_scale, sky, sky_new, scratch):
-    (rim_in, stacked, outgoing, incoming, line_out, line_in), sems = scratch
+    ends = (pl.ds(0, HALO), pl.ds(HALO + HEIGHT, HALO))
+    edges = (pl.ds(0, HALO), pl.ds(HEIGHT - HALO, HALO))
+
+    def pair(side, to):
+        coming = ends[1 - side]
+        return (
+            remote(
+                coeffs_far.at[:, :, edges[side]], coeffs.at[:, :, coming],
+                hs.at[side, 0], hr.at[1 - side, 0], {"sub": to},
+            ),
+            remote(
+                observed_far.at[:, edges[side]], observed.at[:, coming],
+                hs.at[side, 1], hr.at[1 - side, 1], {"sub": to},
+            ),
+        )
+
+    up, down = pair(0, y - 1), pair(1, y + 1)
+
+    def start():
+        @pl.when(y > 0)
+        def _():
+            for copy in up:
+                copy.start()
+
+        @pl.when(y < bands - 1)
+        def _():
+            for copy in down:
+                copy.start()
+
+        @pl.when(y == 0)
+        def _():
+            coeffs[:, :, ends[0]] = jnp.zeros((PIECES, MODES, HALO, BREADTH), jnp.bfloat16)
+            observed[:, ends[0]] = jnp.zeros((PIECES, HALO, BREADTH), jnp.float32)
+
+        @pl.when(y == bands - 1)
+        def _():
+            coeffs[:, :, ends[1]] = jnp.zeros((PIECES, MODES, HALO, BREADTH), jnp.bfloat16)
+            observed[:, ends[1]] = jnp.zeros((PIECES, HALO, BREADTH), jnp.float32)
+
+    def wait():
+        @pl.when(y > 0)
+        def _():
+            for copy in down:
+                copy.wait_recv()
+            for copy in up:
+                copy.wait_send()
+
+        @pl.when(y < bands - 1)
+        def _():
+            for copy in up:
+                copy.wait_recv()
+            for copy in down:
+                copy.wait_send()
+
+    return start, wait
+
+
+def reduce_patches(rows, select, marks, get_scale, sky, sky_new, scratch):
+    (stacked, outgoing, incoming, line_out, line_in), sems = scratch
     axs, axr, bzs, bzr = sems
-    up, down = rims
-    _, x, c, y = place()
-    bands = lax.axis_size("sub")
+    _, x, c, _ = place()
     col = x * NC + c
-    strips = range(PIECES * QCOLS)
-
-    @pl.when(y > 0)
-    def _():
-        down.wait_recv()
-        for n in strips:
-            rows[n, HALO:2 * HALO, :] += rim_in[0, n].astype(jnp.float32)
-
-    @pl.when(y < bands - 1)
-    def _():
-        up.wait_recv()
-        for n in strips:
-            rows[n, HEIGHT:HALO + HEIGHT, :] += rim_in[1, n].astype(jnp.float32)
-
-    for n in strips:
+    for n in range(PIECES * QCOLS):
         for i in range(PH):
-            lines = rows[n, pl.ds(HALO + i, ROWS, stride=PH), :]
+            lines = rows[n, pl.ds(i, ROWS, stride=PH), :]
             stacked[n * ROWS:(n + 1) * ROWS, i * PW:(i + 1) * PW] = lines.astype(jnp.bfloat16)
 
     def exchange(chunk, dx, dc, back):
@@ -341,14 +368,6 @@
     for rel in range(1, NZ):
         along_line(line_out, line_in, bzs, bzr, rel).wait_send()
 
-    @pl.when(y > 0)
-    def _():
-        up.wait_send()
-
-    @pl.when(y < bands - 1)
-    def _():
-        down.wait_send()
-
 
 def own_tile(sky, table):
     z, x, c, _ = place()
@@ -389,22 +408,18 @@
     base[...] = lag_rows(vert, lambda lane: lane - HALO + MARGIN)
 
     def one(m, carry):
-        rows = diagonals(base[pl.ds(m, 1), :], HEIGHT)
-        tall[pl.ds(pl.multiple_of(m * HEIGHT, HEIGHT), HEIGHT), :] = rows[:, :EXT].astype(jnp.bfloat16)
+        rows = diagonals(base[pl.ds(m, 1), :], TALL)
+        tall[pl.ds(pl.multiple_of(m * TALL, TALL), TALL), :] = rows[:, :EXT].astype(jnp.bfloat16)
         return carry
 
     lax.fori_loop(0, MODES, one, 0)
 
 
 def build_wide(vert, base, wide):
-    base[...] = lag_rows(vert, lambda lane: MARGIN - HALO - wrapped(lane))
-
-    def one(m, carry):
-        rows = diagonals(base[pl.ds(m, 1), :], EXT)
-        wide[m] = rows[:, :HEIGHT].astype(jnp.bfloat16)
-        return carry
-
-    lax.fori_loop(0, MODES, one, 0)
+    base[...] = lag_rows(vert, lambda lane: HALO + MARGIN - lane)
+    for m in range(MODES):
+        rows = diagonals(base[m:m + 1, :], HEIGHT)
+        wide[:, m * TALL:(m + 1) * TALL] = rows[:, :TALL].astype(jnp.bfloat16)
 
 
 def build_bands(horiz, base, bands, seams):
@@ -466,8 +481,8 @@
     smooth, back, model = scratch
     for p in range(PIECES):
         for m in range(MODES):
-            smooth[m, p * HEIGHT:(p + 1) * HEIGHT, :] = jnp.dot(
-                tall[m * HEIGHT:(m + 1) * HEIGHT, :], ext[p], preferred_element_type=jnp.float32
+            smooth[m, p * TALL:(p + 1) * TALL, :] = jnp.dot(
+                tall[m * TALL:(m + 1) * TALL, :], ext[p], preferred_element_type=jnp.float32
             ).astype(jnp.bfloat16)
     model[...] = -observed[...]
 
@@ -477,35 +492,36 @@
             cols = slice(q * PW, (q + 1) * PW)
             for p in range(PIECES):
                 model[p, :, cols] += (
-                    coeffs[p, m, :, cols].astype(jnp.float32) * parts[q][p * HEIGHT:(p + 1) * HEIGHT]
+                    coeffs[p, m, :, cols].astype(jnp.float32) * parts[q][p * TALL:(p + 1) * TALL]
                 )
         return carry
 
     lax.fori_loop(0, MODES, forward, 0, unroll=MODES)
-    clipped[...] = jnp.clip(model[...], -DELTA, DELTA)
+    model[...] = jnp.clip(model[...], -DELTA, DELTA)
+    if clipped is not None:
+        clipped[...] = model[:, HALO:HALO + HEIGHT, :]
 
     def adjoint(m, carry):
         weighted = jnp.concatenate(
             [
-                (coeffs[p, m].astype(jnp.float32) * clipped[p]).astype(jnp.bfloat16)
+                (coeffs[p, m].astype(jnp.float32) * model[p]).astype(jnp.bfloat16)
                 for p in range(PIECES)
             ],
             axis=0,
         )
         parts = convolve(weighted, bands[m], seams[m], True)
-        start = pl.multiple_of(m * HEIGHT, HEIGHT)
+        start = pl.multiple_of(m * TALL, TALL)
         for q in range(QCOLS):
             cols = slice(q * PW, (q + 1) * PW)
             for p in range(PIECES):
-                back[p, pl.ds(start, HEIGHT), cols] = parts[q][p * HEIGHT:(p + 1) * HEIGHT].astype(
+                back[p, pl.ds(start, TALL), cols] = parts[q][p * TALL:(p + 1) * TALL].astype(
                     jnp.bfloat16
                 )
         return carry
 
     lax.fori_loop(0, MODES, adjoint, 0, unroll=MODES)
-    turned = jnp.concatenate([wide[m] for m in range(MODES)], axis=1)
     for p in range(PIECES):
-        total = jnp.dot(turned, back[p], preferred_element_type=jnp.float32)
+        total = jnp.dot(wide[...], back[p], preferred_element_type=jnp.float32)
         for q in range(QCOLS):
             rows[p * QCOLS + q] = total[:, q * PW:(q + 1) * PW]
 
@@ -514,14 +530,16 @@
     (
         coeffs, observed, base, tall, wide, bands, seams, own_rows, off_rows, select, extra,
         table, rim_out, rim_in, ext, smooth, back, model, rows, sky_mid,
-        marks_out, marks_in, marks, count_out, count_in, scale, adj_out, *scratch
+        marks_out, marks_in, marks, count_out, count_in, scale, *scratch
     ) = scratch
-    load, mark_sems, fetch_sems = scratch[0], scratch[1:5], scratch[5:13]
-    adj_in, reduce_refs, reduce_sems = scratch[13], scratch[13:19], scratch[19:]
+    load, share_sems, mark_sems, fetch_sems = scratch[0], scratch[1:3], scratch[3:7], scratch[7:15]
+    reduce_refs, reduce_sems = scratch[15:20], scratch[20:]
+    inner = pl.ds(HALO, HEIGHT)
     loads = [
-        pltpu.make_async_copy(coeffs_far, coeffs, load.at[0]),
-        pltpu.make_async_copy(observed_far, observed, load.at[1]),
+        pltpu.make_async_copy(coeffs_far, coeffs.at[:, :, inner], load.at[0]),
+        pltpu.make_async_copy(observed_far, observed.at[:, inner], load.at[1]),
     ]
+    share, shared = share_rows(coeffs_far, observed_far, coeffs, observed, *share_sems)
     all_here = greet()
     for copy in loads:
         copy.start()
@@ -530,6 +548,7 @@
     all_here()
 
     def early():
+        share()
         build_wide(vert, base, wide)
 
     def late():
@@ -543,14 +562,15 @@
         first = step == 0
         sems = [ref.at[step] for ref in fetch_sems]
         spread_tiles(table, sems[:6], early if first else nothing, late if first else nothing)
-        fetch_image(owners, offsets, table, ext, rim_out, rim_in, *sems[6:])
+        fetch_image(owners, offsets, table, ext, rim_out, rim_in.at[step], *sems[6:])
         if first:
             send_marks(select, extra, marks_out, marks_in, *mark_sems[:2])
             for copy in loads:
                 copy.wait()
-        compute(ext, coeffs, observed, (tall, wide, bands, seams), clipped, rows, (smooth, back, model))
+            shared()
+        tables = (tall, wide, bands, seams)
+        compute(ext, coeffs, observed, tables, None if first else clipped, rows, (smooth, back, model))
         sems = [ref.at[step] for ref in reduce_sems]
-        rims = send_rims(rows, adj_out, adj_in, *sems[:2])
         if first:
             take_marks(marks_out, marks_in, marks, count_out, count_in, mark_sems)
 
@@ -560,7 +580,7 @@
             return scale[...]
 
         before, after = (sky, sky_mid) if first else (sky_mid, sky_out)
-        reduce_patches(rows, rims, select, marks, get_scale, before, after, (reduce_refs, sems[2:]))
+        reduce_patches(rows, select, marks, get_scale, before, after, (reduce_refs, sems))
         if first:
             own_tile(sky_mid, table)
 
@@ -585,11 +605,11 @@
     count = PIECES * QCOLS * ROWS
     dma = pltpu.SemaphoreType.DMA
     scratch = [
-        pltpu.VMEM(coeffs.shape, bf16),
-        pltpu.VMEM(observed.shape, f32),
+        pltpu.VMEM((PIECES, MODES, TALL, BREADTH), bf16),
+        pltpu.VMEM((PIECES, TALL, BREADTH), f32),
         pltpu.VMEM((MODES, side), f32),
-        pltpu.VMEM((MODES * HEIGHT, EXT), bf16),
-        pltpu.VMEM((MODES, EXT, HEIGHT), bf16),
+        pltpu.VMEM((MODES * TALL, EXT), bf16),
+        pltpu.VMEM((HEIGHT, MODES * TALL), bf16),
         pltpu.VMEM((MODES, side, side), bf16),
         pltpu.VMEM((MODES, side, side), bf16),
         pltpu.VMEM((count, PW), i32),
@@ -597,13 +617,13 @@
         pltpu.VMEM((N_CHUNKS, COLS * CHUNK_ROWS, count), bf16),
         pltpu.VMEM((count, PW), bf16),
         pltpu.VMEM((COLS * NZ * PER_TILE, PH, PW), bf16),
-        pltpu.VMEM((2, PIECES, HALO, BREADTH), bf16),
-        pltpu.VMEM((2, PIECES, HALO, BREADTH), bf16),
+        pltpu.VMEM((2, PIECES, REACH, BREADTH), bf16),
+        pltpu.VMEM((STEPS, 2, PIECES, REACH, BREADTH), bf16),
         pltpu.VMEM((PIECES, EXT, BREADTH), bf16),
-        pltpu.VMEM((MODES, PIECES * HEIGHT, BREADTH), bf16),
-        pltpu.VMEM((PIECES, MODES * HEIGHT, BREADTH), bf16),
-        pltpu.VMEM((PIECES, HEIGHT, BREADTH), f32),
-        pltpu.VMEM((PIECES * QCOLS, EXT, PW), f32),
+        pltpu.VMEM((MODES, PIECES * TALL, BREADTH), bf16),
+        pltpu.VMEM((PIECES, MODES * TALL, BREADTH), bf16),
+        pltpu.VMEM((PIECES, TALL, BREADTH), f32),
+        pltpu.VMEM((PIECES * QCOLS, HEIGHT, PW), f32),
         pltpu.VMEM((PER_TILE * PH, PW), f32),
         pltpu.VMEM((N_CHUNKS, COLS, CHUNK_ROWS, PW), bf16),
         pltpu.VMEM((N_CHUNKS, COLS, CHUNK_ROWS, PW), bf16),
@@ -611,8 +631,9 @@
         pltpu.VMEM((NZ, PER_TILE, PW), f32),
         pltpu.VMEM((NZ, PER_TILE, PW), f32),
         pltpu.VMEM((PER_TILE, PW), f32),
-        pltpu.VMEM((2, PIECES * QCOLS, HALO, PW), bf16),
         dma((2,)),
+        dma((2, 2)),
+        dma((2, 2)),
         dma((NX, NC)),
         dma((NX, NC)),
         dma((NZ,)),
@@ -625,14 +646,11 @@
         dma((STEPS, NZ, NX)),
         dma((STEPS, 2)),
         dma((STEPS, 2)),
-        pltpu.VMEM((2, PIECES * QCOLS, HALO, PW), bf16),
         pltpu.VMEM((count, SIZE), bf16),
         pltpu.VMEM((N_CHUNKS, COLS, CHUNK_ROWS, SIZE), bf16),
         pltpu.VMEM((N_CHUNKS, COLS, CHUNK_ROWS, SIZE), bf16),
         pltpu.VMEM((NZ, PER_TILE, SIZE), bf16),
         pltpu.VMEM((NZ, PER_TILE, SIZE), bf16),
-        dma((STEPS, 2)),
-        dma((STEPS, 2)),
         dma((STEPS, N_CHUNKS, NX, NC)),
         dma((STEPS, N_CHUNKS, NX, NC)),
         dma((STEPS, NZ)),

time: 85 us -> 83.3 us (0.980)
  Pallas kernels: 84.2 us -> 82.4 us
    pallas_call x1, Pallas kernels: 82.3 us -> 80.5 us  [per_device(): pl.pallas_call(kernel, out_shape=(jax.ShapeDtypeStruct(sky.shape, f32), j...]
where the time goes in v5:
time: 83.3 us; the launch traced here: 83.2 us
  Pallas kernels  82.4 us (99%)
    pallas_call x1, Pallas kernels, per_device(): pl.pallas_call(kernel, out_shape=(jax.ShapeDtypeStruct(sky.shape, f32), j...  80.5 us
    pallas_call x1, Pallas kernels, per_device(): pl.pallas_call(copy_out, out_shape=(jax.ShapeDtypeStruct(sky.shape, f32),...  1.87 us

profile of v5, /device:TPU:1, one launch (start us, length us, event | category | flops | bytes accessed | tf_op | source)
XLA Modules:
  0.0 83.2 jit_solution(1218274289129339029)
XLA Ops:
  0.6 80.5 %shard_map.86 = (f32[64,128]{1,0:T(8,128)}, f32[2,128,512]{2,1,0:T(8,128)}) custom-call(s32[2,4,1,16]{3,2,1,0:T(1,128)} %bitcast.5, s32[2,4,16]{2,1,0:T(4,128)} %bitcast.6, f32[64,128]{1,0:T(8,128)} %bitcast.4, bf16[2,12,128,512]{3,2,1,0:T(8,128)(2,1)} %coeffs_far.1, f32[2,128,512]{2,1,0:T(8,128)} %observed_far.1, bf16[12,21]{1,0:T(8,128)(2,1)} %vert.1, ...), custom_call_target="tpu_custom_call" | custom-call | tf_op jit(solution)/shard_map/pallas_call | solution.py:660
  81.1 1.9 %shard_map.87 = (f32[64,128]{1,0:T(8,128)}, f32[2,128,512]{2,1,0:T(8,128)}) custom-call(f32[64,128]{1,0:T(8,128)} %get-tuple-element.6.sky_far, f32[2,128,512]{2,1,0:T(8,128)} %get-tuple-element.7.clipped_far), custom_call_target="tpu_custom_call" | custom-call | tf_op jit(solution)/shard_map/pallas_call | solution.py:673

commit v6 on v5

--- a/solution.py
+++ b/solution.py
@@ -122,13 +122,17 @@
     for dz in NEAR_ORDER:
         for dx in range(NX):
             to_twin(dz, dx, True).wait_recv()
-    for dz in range(NZ):
-        if dz > 0:
-            along_z(dz, False).wait_send()
-        for dx in range(NX):
-            if dx > 0:
-                along_x(dz, dx, False).wait_send()
-            to_twin(dz, dx, False).wait_send()
+
+    def sent():
+        for dz in range(NZ):
+            if dz > 0:
+                along_z(dz, False).wait_send()
+            for dx in range(NX):
+                if dx > 0:
+                    along_x(dz, dx, False).wait_send()
+                to_twin(dz, dx, False).wait_send()
+
+    return sent
 
 
 def gather_rows(owners, offsets, table, ext, pair):
@@ -148,7 +152,7 @@
             ext[p, pl.ds(start, 2 * PH), q * PW:(q + 1) * PW] = block
 
 
-def fetch_image(owners, offsets, table, ext, rim_out, rim_in, hs, hr):
+def fetch_image(owners, offsets, table, ext, rim_out, rim_in, hs, hr, meanwhile):
     _, _, _, y = place()
     bands = lax.axis_size("sub")
     pairs = ROWS // 2
@@ -172,6 +176,8 @@
         return carry
 
     lax.fori_loop(2, pairs - 2, more, 0)
+    for finish in meanwhile:
+        finish()
     none = jnp.zeros((PIECES, REACH, BREADTH), jnp.bfloat16)
 
     @pl.when(y > 0)
@@ -247,12 +253,12 @@
             count_out[rel] = many[pos * PER_TILE:(pos + 1) * PER_TILE]
     for rel in FAR_ORDER:
         along_line(count_out, count_in, line_send, line_recv, rel).start()
+
+
+def take_counts(marks_out, marks_in, count_out, count_in, scale, sems):
+    send_sem, recv_sem, line_send, line_recv = sems
     for dx, dc in PEERS:
         across(marks_out, marks_in, send_sem, recv_sem, dx, dc, False, True).wait_send()
-
-
-def take_counts(count_out, count_in, scale, sems):
-    _, _, line_send, line_recv = sems
     total = count_out[0]
     for rel in NEAR_ORDER[1:]:
         along_line(count_out, count_in, line_send, line_recv, rel).wait_recv()
@@ -355,6 +361,9 @@
             if rel > 0:
                 along_line(line_out, line_in, bzs, bzr, rel).start()
     scale = get_scale()
+    for chunk in range(N_CHUNKS):
+        for dx, dc in PEERS:
+            exchange(chunk, dx, dc, False).wait_send()
     total = line_out[0].astype(jnp.float32)
     for rel in NEAR_ORDER[1:]:
         along_line(line_out, line_in, bzs, bzr, rel).wait_recv()
@@ -362,11 +371,12 @@
     for i in range(PH):
         old = sky[pl.ds(i, PER_TILE, stride=PH), :]
         sky_new[pl.ds(i, PER_TILE, stride=PH), :] = old - scale * total[:, i * PW:(i + 1) * PW]
-    for chunk in range(N_CHUNKS):
-        for dx, dc in PEERS:
-            exchange(chunk, dx, dc, False).wait_send()
-    for rel in range(1, NZ):
-        along_line(line_out, line_in, bzs, bzr, rel).wait_send()
+
+    def sent():
+        for rel in range(1, NZ):
+            along_line(line_out, line_in, bzs, bzr, rel).wait_send()
+
+    return sent
 
 
 def own_tile(sky, table):
@@ -558,11 +568,12 @@
     def nothing():
         pass
 
+    meanwhile = []
     for step in range(STEPS):
         first = step == 0
         sems = [ref.at[step] for ref in fetch_sems]
-        spread_tiles(table, sems[:6], early if first else nothing, late if first else nothing)
-        fetch_image(owners, offsets, table, ext, rim_out, rim_in.at[step], *sems[6:])
+        sent = spread_tiles(table, sems[:6], early if first else nothing, late if first else nothing)
+        fetch_image(owners, offsets, table, ext, rim_out, rim_in.at[step], *sems[6:], meanwhile + [sent])
         if first:
             send_marks(select, extra, marks_out, marks_in, *mark_sems[:2])
             for copy in loads:
@@ -576,13 +587,16 @@
 
         def get_scale():
             if first:
-                take_counts(count_out, count_in, scale, mark_sems)
+                take_counts(marks_out, marks_in, count_out, count_in, scale, mark_sems)
             return scale[...]
 
         before, after = (sky, sky_mid) if first else (sky_mid, sky_out)
-        reduce_patches(rows, select, marks, get_scale, before, after, (reduce_refs, sems))
+        sent = reduce_patches(rows, select, marks, get_scale, before, after, (reduce_refs, sems))
         if first:
             own_tile(sky_mid, table)
+            meanwhile = [sent]
+        else:
+            sent()
 
 
 def copy_out(sky_far, clipped_far, sky_out, clipped_out, sky, clipped, load, store):

time: 83.3 us -> 83.1 us (level)
  no operation moved by 1% of the time
where the time goes in v6:
time: 83.1 us; the launch traced here: 82.9 us
  Pallas kernels  82.1 us (99%)
    pallas_call x1, Pallas kernels, per_device(): pl.pallas_call(kernel, out_shape=(jax.ShapeDtypeStruct(sky.shape, f32), j...  80.3 us
    pallas_call x1, Pallas kernels, per_device(): pl.pallas_call(copy_out, out_shape=(jax.ShapeDtypeStruct(sky.shape, f32),...  1.87 us

profile of v6, /device:TPU:1, one launch (start us, length us, event | category | flops | bytes accessed | tf_op | source)
XLA Modules:
  0.0 82.9 jit_solution(17632610963970901364)
XLA Ops:
  0.6 80.3 %shard_map.86 = (f32[64,128]{1,0:T(8,128)}, f32[2,128,512]{2,1,0:T(8,128)}) custom-call(s32[2,4,1,16]{3,2,1,0:T(1,128)} %bitcast.5, s32[2,4,16]{2,1,0:T(4,128)} %bitcast.6, f32[64,128]{1,0:T(8,128)} %bitcast.4, bf16[2,12,128,512]{3,2,1,0:T(8,128)(2,1)} %coeffs_far.1, f32[2,128,512]{2,1,0:T(8,128)} %observed_far.1, bf16[12,21]{1,0:T(8,128)(2,1)} %vert.1, ...), custom_call_target="tpu_custom_call" | custom-call | tf_op jit(solution)/shard_map/pallas_call | solution.py:674
  80.9 1.9 %shard_map.87 = (f32[64,128]{1,0:T(8,128)}, f32[2,128,512]{2,1,0:T(8,128)}) custom-call(f32[64,128]{1,0:T(8,128)} %get-tuple-element.6.sky_far, f32[2,128,512]{2,1,0:T(8,128)} %get-tuple-element.7.clipped_far), custom_call_target="tpu_custom_call" | custom-call | tf_op jit(solution)/shard_map/pallas_call | solution.py:687

commit v7 on v6

--- a/solution.py
+++ b/solution.py
@@ -178,33 +178,37 @@
     lax.fori_loop(2, pairs - 2, more, 0)
     for finish in meanwhile:
         finish()
-    none = jnp.zeros((PIECES, REACH, BREADTH), jnp.bfloat16)
-
-    @pl.when(y > 0)
-    def _():
-        down.wait_recv()
-        ext[:, 0:REACH, :] = rim_in[0]
-
-    @pl.when(y == 0)
-    def _():
-        ext[:, 0:REACH, :] = none
-
-    @pl.when(y < bands - 1)
-    def _():
-        up.wait_recv()
-        ext[:, REACH + HEIGHT:EXT, :] = rim_in[1]
-
-    @pl.when(y == bands - 1)
-    def _():
-        ext[:, REACH + HEIGHT:EXT, :] = none
-
-    @pl.when(y > 0)
-    def _():
-        up.wait_send()
-
-    @pl.when(y < bands - 1)
-    def _():
-        down.wait_send()
+
+    def arrive():
+        none = jnp.zeros((PIECES, REACH, BREADTH), jnp.bfloat16)
+
+        @pl.when(y > 0)
+        def _():
+            down.wait_recv()
+            ext[:, 0:REACH, :] = rim_in[0]
+
+        @pl.when(y == 0)
+        def _():
+            ext[:, 0:REACH, :] = none
+
+        @pl.when(y < bands - 1)
+        def _():
+            up.wait_recv()
+            ext[:, REACH + HEIGHT:EXT, :] = rim_in[1]
+
+        @pl.when(y == bands - 1)
+        def _():
+            ext[:, REACH + HEIGHT:EXT, :] = none
+
+        @pl.when(y > 0)
+        def _():
+            up.wait_send()
+
+        @pl.when(y < bands - 1)
+        def _():
+            down.wait_send()
+
+    return arrive
 
 
 def across(outgoing, incoming, send_sem, recv_sem, dx, dc, back, every=False):
@@ -486,27 +490,44 @@
     extra[...] = (mark == along).astype(jnp.bfloat16)
 
 
-def compute(ext, coeffs, observed, tables, clipped, rows, scratch):
+def compute(ext, coeffs, observed, tables, clipped, rows, scratch, arrive):
     tall, wide, bands, seams = tables
     smooth, back, model = scratch
-    for p in range(PIECES):
-        for m in range(MODES):
-            smooth[m, p * TALL:(p + 1) * TALL, :] = jnp.dot(
-                tall[m * TALL:(m + 1) * TALL, :], ext[p], preferred_element_type=jnp.float32
-            ).astype(jnp.bfloat16)
     model[...] = -observed[...]
 
-    def forward(m, carry):
-        parts = convolve(smooth[m], bands[m], seams[m], False)
-        for q in range(QCOLS):
-            cols = slice(q * PW, (q + 1) * PW)
-            for p in range(PIECES):
-                model[p, :, cols] += (
-                    coeffs[p, m, :, cols].astype(jnp.float32) * parts[q][p * TALL:(p + 1) * TALL]
-                )
-        return carry
-
-    lax.fori_loop(0, MODES, forward, 0, unroll=MODES)
+    def ahead(ranges):
+        lengths = [b - a for a, b in ranges]
+        starts = [sum(lengths[:i]) for i in range(len(ranges))]
+        for p in range(PIECES):
+            for m in range(MODES):
+                lines = [tall[m * TALL + a:m * TALL + b, :] for a, b in ranges]
+                result = jnp.dot(
+                    jnp.concatenate(lines, axis=0), ext[p], preferred_element_type=jnp.float32
+                ).astype(jnp.bfloat16)
+                for (a, b), at in zip(ranges, starts):
+                    smooth[m, p * TALL + a:p * TALL + b, :] = result[at:at + b - a]
+
+        def forward(m, carry):
+            block = jnp.concatenate(
+                [smooth[m, p * TALL + a:p * TALL + b, :] for p in range(PIECES) for a, b in ranges],
+                axis=0,
+            )
+            parts = convolve(block, bands[m], seams[m], False)
+            for q in range(QCOLS):
+                cols = slice(q * PW, (q + 1) * PW)
+                for p in range(PIECES):
+                    for (a, b), at in zip(ranges, starts):
+                        at = at + p * sum(lengths)
+                        model[p, a:b, cols] += (
+                            coeffs[p, m, a:b, cols].astype(jnp.float32) * parts[q][at:at + b - a]
+                        )
+            return carry
+
+        lax.fori_loop(0, MODES, forward, 0, unroll=MODES)
+
+    ahead(((REACH, HEIGHT),))
+    arrive()
+    ahead(((0, REACH), (HEIGHT, TALL)))
     model[...] = jnp.clip(model[...], -DELTA, DELTA)
     if clipped is not None:
         clipped[...] = model[:, HALO:HALO + HEIGHT, :]
@@ -554,6 +575,8 @@
     for copy in loads:
         copy.start()
     own_tile(sky, table)
+    for rim in (slice(0, REACH), slice(REACH + HEIGHT, EXT)):
+        ext[:, rim, :] = jnp.zeros((PIECES, REACH, BREADTH), jnp.bfloat16)
     build_tall(vert, base, tall)
     all_here()
 
@@ -573,14 +596,14 @@
         first = step == 0
         sems = [ref.at[step] for ref in fetch_sems]
         sent = spread_tiles(table, sems[:6], early if first else nothing, late if first else nothing)
-        fetch_image(owners, offsets, table, ext, rim_out, rim_in.at[step], *sems[6:], meanwhile + [sent])
+        arrive = fetch_image(owners, offsets, table, ext, rim_out, rim_in.at[step], *sems[6:], meanwhile + [sent])
         if first:
             send_marks(select, extra, marks_out, marks_in, *mark_sems[:2])
             for copy in loads:
                 copy.wait()
             shared()
         tables = (tall, wide, bands, seams)
-        compute(ext, coeffs, observed, tables, None if first else clipped, rows, (smooth, back, model))
+        compute(ext, coeffs, observed, tables, None if first else clipped, rows, (smooth, back, model), arrive)
         sems = [ref.at[step] for ref in reduce_sems]
         if first:
             take_marks(marks_out, marks_in, marks, count_out, count_in, mark_sems)

time: 83.1 us -> 79.9 us (0.961)
  Pallas kernels: 82.1 us -> 78.9 us
    pallas_call x1, Pallas kernels: 80.3 us -> 77 us  [per_device(): pl.pallas_call(kernel, out_shape=(jax.ShapeDtypeStruct(sky.shape, f32), j...]
where the time goes in v7:
time: 79.9 us; the launch traced here: 79.7 us
  Pallas kernels  78.9 us (99%)
  between operations  0.8 us (1%)
    pallas_call x1, Pallas kernels, per_device(): pl.pallas_call(kernel, out_shape=(jax.ShapeDtypeStruct(sky.shape, f32), j...  77 us
    pallas_call x1, Pallas kernels, per_device(): pl.pallas_call(copy_out, out_shape=(jax.ShapeDtypeStruct(sky.shape, f32),...  1.87 us

profile of v7, /device:TPU:1, one launch (start us, length us, event | category | flops | bytes accessed | tf_op | source)
XLA Modules:
  0.0 79.7 jit_solution(9108875857907175977)
XLA Ops:
  0.6 77.0 %shard_map.86 = (f32[64,128]{1,0:T(8,128)}, f32[2,128,512]{2,1,0:T(8,128)}) custom-call(s32[2,4,1,16]{3,2,1,0:T(1,128)} %bitcast.5, s32[2,4,16]{2,1,0:T(4,128)} %bitcast.6, f32[64,128]{1,0:T(8,128)} %bitcast.4, bf16[2,12,128,512]{3,2,1,0:T(8,128)(2,1)} %coeffs_far.1, f32[2,128,512]{2,1,0:T(8,128)} %observed_far.1, bf16[12,21]{1,0:T(8,128)(2,1)} %vert.1, ...), custom_call_target="tpu_custom_call" | custom-call | tf_op jit(solution)/shard_map/pallas_call | solution.py:697
  77.7 1.9 %shard_map.87 = (f32[64,128]{1,0:T(8,128)}, f32[2,128,512]{2,1,0:T(8,128)}) custom-call(f32[64,128]{1,0:T(8,128)} %get-tuple-element.6.sky_far, f32[2,128,512]{2,1,0:T(8,128)} %get-tuple-element.7.clipped_far), custom_call_target="tpu_custom_call" | custom-call | tf_op jit(solution)/shard_map/pallas_call | solution.py:710
